TPU v7x, 512 devices: a whole 4x8x8 slice. The times are simulated.
512 devices in a mesh: gx: 32 (over x, z), gy: 4 (over y_hi, core), dp: 4 (over y_lo).
Axes of the slice: x: 4, y: 8 (y_hi: 2, y_lo: 4; y = y_hi * 4 + y_lo), z: 8, core: 2. Of those that a mesh axis runs over, the one named last changes fastest.
Arguments:
- features: bfloat16 [4, 512, 1024, 128], P('dp', 'gx', 'gy'), may hold values from -6 to 6
- kernel: bfloat16 [3, 3, 3, 64, 64], replicated, may hold values from -0.15625 to 0.15625
- offsets: float32 [64], replicated, may hold values from -3 to 3
- upstream: bfloat16 [4, 512, 1024, 128], P('dp', 'gx', 'gy'), may hold values from -6 to 6
- grad_exponents: int32 [3, 3, 3], replicated, may hold values from -2 to 2
Outputs:
- activation: bfloat16 [4, 512, 1024, 128], P('dp', 'gx', 'gy')
- input_grad: bfloat16 [4, 512, 1024, 128], P('dp', 'gx', 'gy')
- kernel_grad: bfloat16 [3, 3, 3, 64, 64], P(None, None, None, None, 'dp')
- bias_grad: float32 [64], P('dp')
All inputs are finite; a program needn't handle non-finite values.
Results may differ from a plain program's by a relative error of at most 0.007.
Values may be sent and summed in bfloat16 or wider, within the bound.
A program may use at most 128 MiB of HBM per device.

v0:
```python
import math

import jax
import jax.numpy as jnp
from jax import lax
from jax.sharding import PartitionSpec as P


def extended(cells, sides, width):
    for axis, dim in sides:
        count = lax.axis_size(axis)
        ends = count - 1
        head = lax.slice_in_dim(cells, 0, width, axis=dim)
        tail = lax.slice_in_dim(cells, cells.shape[dim] - width, cells.shape[dim], axis=dim)
        cells = jnp.concatenate(
            [
                lax.ppermute(tail, axis, [(i, (i + 1) % count) for i in range(ends)]),
                cells,
                lax.ppermute(head, axis, [((i + 1) % count, i) for i in range(ends)]),
            ],
            axis=dim,
        )
    return cells


def build_matrices(kernel):
    upper = jnp.concatenate([kernel[:, :, 1], kernel[:, :, 0]], axis=-1)
    lower = jnp.concatenate([kernel[:, :, 2], kernel[:, :, 1]], axis=-1)
    return jnp.concatenate([upper, lower], axis=2)


def forward_conv(padded, matrices, size_x, size_y, bias_full):
    total = bias_full
    for shift_x in range(3):
        for shift_y in range(3):
            window = padded[:, shift_x : shift_x + size_x, shift_y : shift_y + size_y]
            total = total + jnp.einsum(
                "sxyc,cd->sxyd",
                window,
                matrices[shift_x, shift_y],
                preferred_element_type=jnp.float32,
            )
    return total


def backward_conv(grad_pad, matrices, size_x, size_y):
    total = None
    for shift_x in range(3):
        for shift_y in range(3):
            window = grad_pad[
                :, 2 - shift_x : 2 - shift_x + size_x, 2 - shift_y : 2 - shift_y + size_y
            ]
            term = jnp.einsum(
                "sxyd,cd->sxyc",
                window,
                matrices[shift_x, shift_y],
                preferred_element_type=jnp.float32,
            )
            total = term if total is None else total + term
    return total


def weight_blocks(source_pad, pre_grad, start, size_x, size_y):
    blocks = []
    for shift_x in range(3):
        for shift_y in range(3):
            window = source_pad[
                :,
                start + shift_x : start + shift_x + size_x,
                start + shift_y : start + shift_y + size_y,
            ]
            blocks.append(
                jnp.einsum("sxyc,sxyd->cd", window, pre_grad, preferred_element_type=jnp.float32)
            )
    width = pre_grad.shape[3]
    return jnp.stack(blocks).reshape(3, 3, width, width)


def local(features, kernel, offsets, upstream, grad_exponents):
    matrices = build_matrices(kernel)
    size_x, size_y, width = (features.shape[1], features.shape[2], features.shape[3])
    chans = width // 2
    bias_full = jnp.concatenate([offsets, offsets])
    padded = extended(features, (("gx", 1), ("gy", 2)), 1)
    preact = forward_conv(padded, matrices, size_x, size_y, bias_full)
    sigma = jax.nn.sigmoid(preact)
    activation = (preact * sigma).astype(jnp.bfloat16)
    pre_grad = (upstream.astype(jnp.float32) * sigma * (1.0 + preact * (1.0 - sigma))).astype(
        jnp.bfloat16
    )
    grad_pad = extended(pre_grad, (("gx", 1), ("gy", 2)), 1)
    matrix_grad = weight_blocks(padded, pre_grad, 0, size_x, size_y)
    input_grad = backward_conv(grad_pad, matrices, size_x, size_y).astype(jnp.bfloat16)
    tap_low = matrix_grad[:, :, :chans, chans:]
    tap_mid = matrix_grad[:, :, :chans, :chans] + matrix_grad[:, :, chans:, chans:]
    tap_high = matrix_grad[:, :, chans:, :chans]
    tap_grad = jnp.stack([tap_low, tap_mid, tap_high], axis=2)
    summed = jnp.sum(pre_grad.astype(jnp.float32), axis=(0, 1, 2))
    bias_sum = summed[:chans] + summed[chans:]
    tap_grad, bias_sum = lax.psum((tap_grad, bias_sum), ("gx", "gy"))
    tap_grad, bias_sum = (
        lax.psum_scatter(tap_grad, "dp", scatter_dimension=4, tiled=True),
        lax.psum_scatter(bias_sum, "dp", scatter_dimension=0, tiled=True),
    )
    count = (
        features.shape[0]
        * lax.axis_size("dp")
        * size_x
        * lax.axis_size("gx")
        * size_y
        * lax.axis_size("gy")
        * 2
    )
    inverse = 1.0 / math.sqrt(count)
    scales = jnp.exp2(grad_exponents.astype(jnp.float32))[:, :, :, None, None]
    kernel_grad = (tap_grad * scales * inverse).astype(jnp.bfloat16)
    bias_grad = bias_sum * inverse
    return (activation, input_grad, kernel_grad, bias_grad)


def solution(mesh):
    placed = (P("dp", "gx", "gy", None), P(), P(), P("dp", "gx", "gy", None), P())
    return jax.shard_map(
        local,
        mesh=mesh,
        in_specs=placed,
        out_specs=(
            P("dp", "gx", "gy", None),
            P("dp", "gx", "gy", None),
            P(None, None, None, None, "dp"),
            P("dp"),
        ),
        check_vma=False,
    )
```

profile of v0, /device:TPU:1, one launch (start us, length us, event | category | flops | bytes accessed | tf_op | source)
XLA Modules:
  0.0 1928.5 jit_solution(13702041898073981906)
XLA Ops:
  7.2 1.0 fusion.95
  8.2 4.8 collective-permute-start
  13.0 1.3 collective-permute-start.1
  14.3 0.7 multiply_exponential_fusion
  15.0 1.1 slice_bitcast_fusion.15
  16.3 1.8 fusion.53
  18.1 1.3 dynamic-slice
  20.3 5.3 collective-permute-start.3
  25.6 5.0 collective-permute-start.2
  33.6 1.1 copy-done.1
  35.0 3.6 convert_reduce_fusion
  38.7 9.2 all-reduce
  48.0 409.4 %psum.17 = f32[16]{0:T(128)S(1)} all-reduce(f32[16]{0:T(128)S(1)} %dynamic-slice.1), channel_id=1, replica_groups=mesh['gx'=32,'gy'=4,'dp'=4] {'gx','gy'}, use_global_device_ids=true, to_apply=%region_3.0 | all-reduce | flops 16 | bytes 128 | tf_op jit(solution)/shard_map/psum | solution.py:100
  458.5 1.3 collective-permute-start.5
  459.8 4.0 collective-permute-start.4
  464.3 1.3 fusion.12
  470.0 1.0 pad_maximum_fusion.7
  471.0 3.1 fusion.55
  474.2 1.8 fusion.50
  476.0 1.9 collective-permute-start.7
  477.9 4.2 collective-permute-start.6
  482.1 1.8 fusion.25
  483.9 1.7 fusion.33
  485.6 1.5 collective-permute-done.6
  487.8 1.8 fusion.29
  489.6 1.8 fusion.31
  491.3 1.8 fusion.28
  493.1 1.8 fusion.30
  494.9 1.8 fusion.36
  496.7 7.8 fusion.22
  504.5 1415.5 %all-reduce.3.cloned.1.call-done = f32[3,3,3,64,16]{3,4,2,1,0:T(8,128)} async-done(((f32[3,3,3,64,16]{3,4,2,1,0:T(8,128)}), f32[3,3,3,64,16]{3,4,2,1,0:T(8,128)}) %all-reduce.3.cloned.1.call-update) | async-done | bytes 110608 | tf_op jit(solution)/shard_map/psum | solution.py:100
  1920.0 1.7 multiply_convert_fusion.1
  (58 shorter events, 10.6 us)
Async XLA Ops:
  7.2 9.1 copy-start
  7.2 489.5 %reduce-scatter.2.cloned.1.call-start = ((), (), s32[]{:S(2)}) async-start(), calls=%async_computation.1 | async-start | bytes 1105920 | tf_op jit(solution)/shard_map/reduce_scatter | solution.py:102
  8.2 11.9 collective-permute-start
  13.0 7.3 collective-permute-start.1
  16.1 3.9 copy-start.6
  16.3 16.9 copy-start.2
  20.1 10.9 copy-start.5
  20.3 12.4 collective-permute-start.3
  25.6 5.8 collective-permute-start.2
  33.2 1.6 copy-start.1
  33.2 1.8 copy-start.4
  458.5 17.4 collective-permute-start.5
  459.8 16.1 collective-permute-start.4
  471.0 3.2 copy-start.3
  471.0 1449.0 %all-reduce.3.cloned.1.call-start = ((), (), s32[]{:S(2)}) async-start(), calls=%async_computation.2 | async-start | bytes 442368 | tf_op jit(solution)/shard_map/psum | solution.py:100
  476.0 9.6 collective-permute-start.7
  477.9 9.2 collective-permute-start.6
Sparse Core Ops, SparseCore 0:
  471.1 22.4 reduce-scatter.1
  496.9 1423.0 all-reduce.2
where the time goes:
time: 1930 us
  waiting for transfers between devices  1420 us (74%)
  blocking collectives  419 us (22%)
  matrix products  35.5 us (2%)
  starting transfers between devices  27.8 us (1%)
    psum x1, waiting for transfers between devices, local(): tap_grad, bias_sum = lax.psum((tap_grad, bias_sum), ('gx', 'gy'))  1420 us
    psum x1, blocking collectives, local(): tap_grad, bias_sum = lax.psum((tap_grad, bias_sum), ('gx', 'gy'))  409 us
  transfers between devices with their start and end apart: 10, of which 2 were waited for; matrix products, arithmetic and copies ran while one was open for 2% of the time, Pallas kernels for 0%

commit v1 on v0

--- a/solution.py
+++ b/solution.py
@@ -1,9 +1,14 @@
+import functools
 import math
 
 import jax
 import jax.numpy as jnp
 from jax import lax
+from jax.experimental import pallas as pl
+from jax.experimental.pallas import tpu as pltpu
 from jax.sharding import PartitionSpec as P
+
+MESH = pl.DeviceIdType.MESH
 
 
 def extended(cells, sides, width):
@@ -70,10 +75,139 @@
                 start + shift_y : start + shift_y + size_y,
             ]
             blocks.append(
-                jnp.einsum("sxyc,sxyd->cd", window, pre_grad, preferred_element_type=jnp.float32)
+                jnp.einsum("sxyd,sxyc->dc", pre_grad, window, preferred_element_type=jnp.float32)
             )
-    width = pre_grad.shape[3]
-    return jnp.stack(blocks).reshape(3, 3, width, width)
+    return jnp.stack(blocks)
+
+
+NX, NZ, NH, NC, ND = 4, 8, 2, 2, 4
+NYL = NH * ND
+TILES = 32
+
+
+def place():
+    gx, gy, d = lax.axis_index("gx"), lax.axis_index("gy"), lax.axis_index("dp")
+    return gx // NZ, gx % NZ, gy // NC, gy % NC, d
+
+
+def device(x, z, h, c, d):
+    return {"gx": x * NZ + z, "gy": h * NC + c, "dp": d}
+
+
+def peers(x, z, h, c, d):
+    y = h * ND + d
+    out = []
+    for j in range(1, NC * NX * NH):
+        out.append(device((x + (j // 2) % NX) % NX, z, (h + j // (2 * NX)) % NH, (c + j % 2) % NC, d))
+    for k in range(1, NYL):
+        if k != ND:
+            other = (y + k) % NYL
+            out.append(device(x, z, other // ND, c, other % ND))
+    for k in range(1, NZ):
+        out.append(device(x, (z + k) % NZ, h, c, d))
+    return out
+
+
+def reduce_kernel(
+    v_ref, out_ref, cbuf, xbuf, ybuf, zbuf, acc1, acc2, acc3,
+    csem, xsem, ysem, zsem, gsem,
+):
+    x, z, h, c, d = place()
+    y = h * ND + d
+
+    barrier = pltpu.get_barrier_semaphore()
+    others = peers(x, z, h, c, d)
+    for peer in others:
+        pl.semaphore_signal(barrier, inc=1, device_id=peer, device_id_type=MESH)
+    pl.semaphore_wait(barrier, len(others))
+
+    def send(src, dst, sems, k, peer):
+        copy = pltpu.make_async_remote_copy(
+            src_ref=src, dst_ref=dst, send_sem=sems.at[0, k], recv_sem=sems.at[1, k],
+            device_id=peer, device_id_type=MESH,
+        )
+        copy.start()
+        return copy
+
+    first = send(v_ref.at[1 - c], cbuf, csem, 0, device(x, z, h, 1 - c, d))
+    first.wait_recv()
+    acc1[...] = v_ref[c] + cbuf[...]
+
+    copies_x = [
+        send(acc1.at[(x + k) % NX], xbuf.at[k - 1], xsem, k - 1, device((x + k) % NX, z, h, c, d))
+        for k in range(1, NX)
+    ]
+    for copy in copies_x:
+        copy.wait_recv()
+    acc2[...] = acc1[x] + xbuf[0] + xbuf[1] + xbuf[2]
+
+    copies_y = []
+    for k in range(1, NYL):
+        other = (y + k) % NYL
+        copies_y.append(
+            send(acc2.at[other], ybuf.at[k - 1], ysem, k - 1, device(x, z, other // ND, c, other % ND))
+        )
+    for copy in copies_y:
+        copy.wait_recv()
+    total = acc2[y]
+    for k in range(NYL - 1):
+        total = total + ybuf[k]
+    acc3[...] = total
+    zbuf[z] = total
+
+    copies_z = [
+        send(acc3, zbuf.at[z], zsem, k - 1, device(x, (z + k) % NZ, h, c, d)) for k in range(1, NZ)
+    ]
+    for k in range(1, NZ):
+        source = (z + NZ - k) % NZ
+        pltpu.make_async_remote_copy(
+            src_ref=acc3, dst_ref=zbuf.at[source], send_sem=zsem.at[0, k - 1], recv_sem=zsem.at[1, k - 1],
+            device_id=device(x, source, h, c, d), device_id_type=MESH,
+        ).wait_recv()
+    total = zbuf[0]
+    for k in range(1, NZ):
+        total = total + zbuf[k]
+    out_ref[c, x, h] = total
+
+    copies_g = []
+    for j in range(1, NC * NX * NH):
+        peer = device((x + (j // 2) % NX) % NX, z, (h + j // (2 * NX)) % NH, (c + j % 2) % NC, d)
+        copies_g.append(send(out_ref.at[c, x, h], out_ref.at[c, x, h], gsem, j - 1, peer))
+    for j in range(1, NC * NX * NH):
+        px, ph, pc = (x + NX - (j // 2) % NX) % NX, (h + NH - j // (2 * NX)) % NH, (c + NC - j % 2) % NC
+        pltpu.make_async_remote_copy(
+            src_ref=out_ref.at[pc, px, ph], dst_ref=out_ref.at[pc, px, ph],
+            send_sem=gsem.at[0, j - 1], recv_sem=gsem.at[1, j - 1],
+            device_id=device(px, z, ph, pc, d), device_id_type=MESH,
+        ).wait_recv()
+    for copy in [first] + copies_x + copies_y + copies_z + copies_g:
+        copy.wait_send()
+
+
+def reduced(pieces):
+    f32 = jnp.float32
+    return pl.pallas_call(
+        reduce_kernel,
+        out_shape=jax.ShapeDtypeStruct((NC, NX, NH, 2, 8, 128), f32),
+        in_specs=[pl.BlockSpec(memory_space=pltpu.VMEM)],
+        out_specs=pl.BlockSpec(memory_space=pltpu.VMEM),
+        scratch_shapes=[
+            pltpu.VMEM((NX, NYL, 2, 8, 128), f32),
+            pltpu.VMEM((NX - 1, NYL, 2, 8, 128), f32),
+            pltpu.VMEM((NYL - 1, 2, 8, 128), f32),
+            pltpu.VMEM((NZ, 2, 8, 128), f32),
+            pltpu.VMEM((NX, NYL, 2, 8, 128), f32),
+            pltpu.VMEM((NYL, 2, 8, 128), f32),
+            pltpu.VMEM((2, 8, 128), f32),
+            pltpu.SemaphoreType.DMA((2, 1)),
+            pltpu.SemaphoreType.DMA((2, NX - 1)),
+            pltpu.SemaphoreType.DMA((2, NYL - 1)),
+            pltpu.SemaphoreType.DMA((2, NZ - 1)),
+            pltpu.SemaphoreType.DMA((2, NC * NX * NH - 1)),
+        ],
+        compiler_params=pltpu.CompilerParams(collective_id=0, has_side_effects=True),
+        cost_estimate=pl.CostEstimate(flops=1_000_000, bytes_accessed=40_000_000, transcendentals=0),
+    )(pieces)
 
 
 def local(features, kernel, offsets, upstream, grad_exponents):
@@ -89,19 +223,28 @@
         jnp.bfloat16
     )
     grad_pad = extended(pre_grad, (("gx", 1), ("gy", 2)), 1)
-    matrix_grad = weight_blocks(padded, pre_grad, 0, size_x, size_y)
+    blocks = weight_blocks(padded, pre_grad, 0, size_x, size_y)
     input_grad = backward_conv(grad_pad, matrices, size_x, size_y).astype(jnp.bfloat16)
-    tap_low = matrix_grad[:, :, :chans, chans:]
-    tap_mid = matrix_grad[:, :, :chans, :chans] + matrix_grad[:, :, chans:, chans:]
-    tap_high = matrix_grad[:, :, chans:, :chans]
-    tap_grad = jnp.stack([tap_low, tap_mid, tap_high], axis=2)
     summed = jnp.sum(pre_grad.astype(jnp.float32), axis=(0, 1, 2))
     bias_sum = summed[:chans] + summed[chans:]
-    tap_grad, bias_sum = lax.psum((tap_grad, bias_sum), ("gx", "gy"))
-    tap_grad, bias_sum = (
-        lax.psum_scatter(tap_grad, "dp", scatter_dimension=4, tiled=True),
-        lax.psum_scatter(bias_sum, "dp", scatter_dimension=0, tiled=True),
-    )
+
+    mid = blocks[:, :chans, :chans] + blocks[:, chans:, chans:]
+    both = jnp.concatenate([mid, blocks[:, :chans, chans:]], axis=-1)
+    low = jnp.concatenate(
+        [blocks[:, chans:, :chans], jnp.broadcast_to(bias_sum[None, :, None], (1, chans, chans))]
+    )
+    packed = jnp.concatenate([both, jnp.concatenate([low[0::2], low[1::2]], axis=-1)])
+    pieces = packed.reshape(14, ND, 2, 8, 128).transpose(1, 0, 2, 3, 4).reshape(ND, 28, 8, 128)
+    pieces = jnp.pad(pieces, ((0, 0), (0, TILES - 28), (0, 0), (0, 0)))
+    pieces = pieces.reshape(ND, NC, NX, NH, 2, 8, 128).transpose(1, 2, 3, 0, 4, 5, 6)
+    total = reduced(pieces.reshape(NC, NX, NYL, 2, 8, 128))
+    total = total.reshape(TILES, 8, 128)[:28].reshape(14, 16, 128)
+    own = total.shape[1]
+    low = total[9:].reshape(5, own, 2, chans).transpose(0, 2, 1, 3).reshape(10, own, chans)
+    taps = jnp.stack([low[:9], total[:9, :, :chans], total[:9, :, chans:]], axis=1)
+    tap_grad = taps.reshape(3, 3, 3, own, chans).swapaxes(3, 4)
+    bias_sum = low[9, :, 0]
+
     count = (
         features.shape[0]
         * lax.axis_size("dp")

time: 1930 us -> 118 us (0.06)
  waiting for transfers between devices: 1420 us -> 6.74 us
  blocking collectives: 419 us -> 0 us
  Pallas kernels: 0 us -> 40.5 us
    psum x1 -> x0, waiting for transfers between devices: 1420 us -> none  [local(): tap_grad, bias_sum = lax.psum((tap_grad, bias_sum), ('gx', 'gy'))]
    psum x1 -> x0, blocking collectives: 409 us -> none  [local(): tap_grad, bias_sum = lax.psum((tap_grad, bias_sum), ('gx', 'gy'))]
    pallas_call x0 -> x1, Pallas kernels: none -> 40.5 us  [reduced(): pl.pallas_call(reduce_kernel, out_shape=jax.ShapeDtypeStruct((NC, NX, NH,...]
  transfers between devices with their start and end apart: 10 -> 8, of which waited for: 2 -> 2; matrix products, arithmetic and copies ran while one was open for 2% -> 16% of each run, Pallas kernels for 0% -> 0%
where the time goes in v1:
time: 118 us; the launch traced here: 117 us
  Pallas kernels  40.5 us (34%)
  starting transfers between devices  29.8 us (25%)
  matrix products  17.2 us (15%)
  local copies, waits for them, and re-layouts  13.1 us (11%)
  other arithmetic  8.8 us (7%)
  waiting for transfers between devices  6.74 us (6%)
    pallas_call x1, Pallas kernels, reduced(): pl.pallas_call(reduce_kernel, out_shape=jax.ShapeDtypeStruct((NC, NX, NH,...  40.5 us
    ppermute x4, starting transfers between devices, extended(): lax.ppermute(tail, axis, [(i, (i + 1) % count) for i in range(ends)])  19.4 us
    ppermute x4, starting transfers between devices, extended(): lax.ppermute(head, axis, [((i + 1) % count, i) for i in range(ends)])  10.4 us
    ppermute x4, waiting for transfers between devices, extended(): lax.ppermute(head, axis, [((i + 1) % count, i) for i in range(ends)])  6.73 us
    dot_general x9, matrix products, backward_conv(): jnp.einsum('sxyd,cd->sxyc', window, matrices[shift_x, shift_y], preferred...  6.57 us
    dot_general x9, matrix products, forward_conv(): jnp.einsum('sxyc,cd->sxyd', window, matrices[shift_x, shift_y], preferred...  6.22 us
    dot_general x9, matrix products, weight_blocks(): jnp.einsum('sxyd,sxyc->dc', pre_grad, window, preferred_element_type=jnp....  4.4 us
    slice x2, local copies, waits for them, and re-layouts, local(): low[:9]  3.42 us
  transfers between devices with their start and end apart: 8, of which 2 were waited for; matrix products, arithmetic and copies ran while one was open for 16% of the time, Pallas kernels for 0%

profile of v1, /device:TPU:1, one launch (start us, length us, event | category | flops | bytes accessed | tf_op | source)
XLA Modules:
  0.0 117.0 jit_solution(9882695606519118361)
XLA Ops:
  0.6 1.0 fusion.99
  1.6 4.8 %collective-permute-start = (bf16[1,1,256,128]{3,2,1,0:T(8,128)(2,1)S(1)}, bf16[1,1,256,128]{3,2,1,0:T(8,128)(2,1)S(1)}, u32[]{:S(2)}, u32[]{:S(2)}) collective-permute-start(bf16[1,1,256,128]{3,2,1,0:T(8,128)(2,1)S(1)} %get-tuple-element.14), channel_id=1, source_target_pairs={{0,16},{16,32},{32,48},{48,64},{64,80},{80,96},{96,112},{112,128},... | collective-permute-start | bytes 196616 | tf_op jit(solution)/shard_map/ppermute | solution.py:22
  6.4 1.3 %collective-permute-start.1 = (bf16[1,1,256,128]{3,2,1,0:T(8,128)(2,1)S(1)}, bf16[1,1,256,128]{3,2,1,0:T(8,128)(2,1)S(1)}, u32[]{:S(2)}, u32[]{:S(2)}) collective-permute-start(bf16[1,1,256,128]{3,2,1,0:T(8,128)(2,1)S(1)} %get-tuple-element.15), channel_id=1, source_target_pairs={{16,0},{32,16},{48,32},{64,48},{80,64},{96,80},{112,96},{128,112},... | collective-permute-start | bytes 196616 | tf_op jit(solution)/shard_map/ppermute | solution.py:24
  7.7 0.7 multiply_exponential_fusion
  8.5 1.1 slice_bitcast_fusion.15
  10.4 1.7 %collective-permute-done.1 = bf16[1,1,256,128]{3,2,1,0:T(8,128)(2,1)S(1)} collective-permute-done((bf16[1,1,256,128]{3,2,1,0:T(8,128)(2,1)S(1)}, bf16[1,1,256,128]{3,2,1,0:T(8,128)(2,1)S(1)}, u32[]{:S(2)}, u32[]{:S(2)}) %collective-permute-start.1) | collective-permute-done | bytes 65568 | tf_op jit(solution)/shard_map/ppermute | solution.py:24
  12.1 5.8 %collective-permute-start.3 = (bf16[1,18,1,128]{3,2,1,0:T(2,128)(2,1)S(1)}, bf16[1,18,1,128]{3,2,1,0:T(2,128)(2,1)S(1)}, u32[]{:S(2)}, u32[]{:S(2)}) collective-permute-start(bf16[1,18,1,128]{3,2,1,0:T(2,128)(2,1)S(1)} %get-tuple-element.10), channel_id=1, source_target_pairs={{4,0},{8,4},{12,8},{5,1},{9,5},{13,9},{6,2},{10,6},{14,10},{7,3},{... | collective-permute-start | bytes 13832 | tf_op jit(solution)/shard_map/ppermute | solution.py:24
  17.9 5.3 %collective-permute-start.2 = (bf16[1,18,1,128]{3,2,1,0:T(2,128)(2,1)S(1)}, bf16[1,18,1,128]{3,2,1,0:T(2,128)(2,1)S(1)}, u32[]{:S(2)}, u32[]{:S(2)}) collective-permute-start(bf16[1,18,1,128]{3,2,1,0:T(2,128)(2,1)S(1)} %get-tuple-element.11), channel_id=1, source_target_pairs={{0,4},{4,8},{8,12},{1,5},{5,9},{9,13},{2,6},{6,10},{10,14},{3,7},{... | collective-permute-start | bytes 13832 | tf_op jit(solution)/shard_map/ppermute | solution.py:22
  26.3 0.8 copy-done.1
  27.1 2.8 %convert_reduce_fusion = (f32[128]{0:T(128)S(1)}, bf16[1,16,256,128]{3,2,1,0:T(8,128)(2,1)S(1)}, f32[16,256,128]{2,1,0:T(8,128)}) fusion(bf16[1,16,256,128]{3,2,1,0:T(8,128)(2,1)S(1)} %copy-done.1, bf16[3,3,128,128]{3,2,1,0:T(8,128)(2,1)S(1)} %maximum_maximum_fusion.2, bf16[1,18,1,128]{3,2,1,0:T(2,128)(2,1)S(1)} %collective-permute-done.3, ...), kind=kOutput, calls=%fused_computation.8 | convolution fusion | flops 147324800 | bytes 22194176 | tf_op jit(solution)/shard_map/sxyc,cd->sxyd/dot_general | solution.py:42
  29.9 0.7 fusion.98
  35.7 0.8 copy.40
  36.5 40.5 %shard_map.84 = f32[2,4,2,2,8,128]{5,4,3,2,1,0:T(8,128)} custom-call(f32[2,4,8,2,8,128]{5,4,3,2,1,0:T(8,128)} %bitcast.247), custom_call_target="tpu_custom_call" | custom-call | flops 1000000 | bytes 40000000 | tf_op jit(solution)/shard_map/pallas_call | solution.py:189
  77.0 0.8 slice.267
  77.8 0.9 slice.269
  79.1 1.3 %collective-permute-start.5 = (bf16[1,1,256,128]{3,2,1,0:T(8,128)(2,1)}, bf16[1,1,256,128]{3,2,1,0:T(8,128)(2,1)S(1)}, u32[]{:S(2)}, u32[]{:S(2)}) collective-permute-start(bf16[1,1,256,128]{3,2,1,0:T(8,128)(2,1)} %get-tuple-element.12), channel_id=1, source_target_pairs={{16,0},{32,16},{48,32},{64,48},{80,64},{96,80},{112,96},{128,112},... | collective-permute-start | bytes 196616 | tf_op jit(solution)/shard_map/ppermute | solution.py:24
  80.4 4.6 %collective-permute-start.4 = (bf16[1,1,256,128]{3,2,1,0:T(8,128)(2,1)}, bf16[1,1,256,128]{3,2,1,0:T(8,128)(2,1)}, u32[]{:S(2)}, u32[]{:S(2)}) collective-permute-start(bf16[1,1,256,128]{3,2,1,0:T(8,128)(2,1)} %get-tuple-element.13), channel_id=1, source_target_pairs={{0,16},{16,32},{32,48},{48,64},{64,80},{80,96},{96,112},{112,128},... | collective-permute-start | bytes 196616 | tf_op jit(solution)/shard_map/ppermute | solution.py:22
  85.0 0.7 fusion.101
  85.7 0.7 reshape.190
  86.5 1.8 %copy.41 = f32[5,16,2,64]{1,3,2,0:T(8,128)} copy(f32[5,16,2,64]{3,2,1,0:T(2,128)} %reshape.190) | data formatting | bytes 81920 | tf_op jit(solution)/shard_map/reshape | solution.py:243
  88.3 1.7 %slice.268 = f32[9,16,64]{1,2,0:T(8,128)} slice(f32[10,16,64]{1,2,0:T(8,128)} %bitcast.250), slice={[0:9], [0:16], [0:64]} | slice | bytes 73728 | tf_op jit(solution)/shard_map/slice | solution.py:244
  89.9 1.7 %copy.42 = f32[9,16,64]{2,1,0:T(8,128)} copy(f32[9,16,64]{1,2,0:T(8,128)} %slice.268) | data formatting | bytes 73728 | tf_op jit(solution)/shard_map/slice | solution.py:244
  91.7 3.2 %fusion.55 = bf16[1,16,256,128]{3,2,1,0:T(8,128)(2,1)} fusion(f32[16,256,128]{2,1,0:T(8,128)} %get-tuple-element.26), kind=kLoop, calls=%fused_computation.91 | loop fusion | flops 2621440 | bytes 3145728 | tf_op jit(solution)/shard_map/convert_element_type | solution.py:221
  94.9 0.7 fusion.72
  95.6 1.2 %fusion.77 = f32[16]{0:T(128)} fusion(f32[10,16,64]{1,2,0:T(8,128)} %bitcast.251), kind=kLoop, calls=%fused_computation.128 | loop fusion | flops 16 | bytes 128 | tf_op jit(solution)/shard_map/mul | solution.py:260
  96.8 0.7 pad_maximum_fusion.8
  97.5 4.6 %collective-permute-start.7 = (bf16[1,18,1,128]{3,2,1,0:T(2,128)(2,1)S(1)}, bf16[1,18,1,128]{3,2,1,0:T(2,128)(2,1)S(1)}, u32[]{:S(2)}, u32[]{:S(2)}) collective-permute-start(bf16[1,18,1,128]{3,2,1,0:T(2,128)(2,1)S(1)} %get-tuple-element.8), channel_id=1, source_target_pairs={{0,4},{4,8},{8,12},{1,5},{5,9},{9,13},{2,6},{6,10},{10,14},{3,7},{... | collective-permute-start | bytes 13832 | tf_op jit(solution)/shard_map/ppermute | solution.py:22
  102.1 2.1 %collective-permute-start.6 = (bf16[1,18,1,128]{3,2,1,0:T(2,128)(2,1)S(1)}, bf16[1,18,1,128]{3,2,1,0:T(2,128)(2,1)S(1)}, u32[]{:S(2)}, u32[]{:S(2)}) collective-permute-start(bf16[1,18,1,128]{3,2,1,0:T(2,128)(2,1)S(1)} %get-tuple-element.9), channel_id=1, source_target_pairs={{4,0},{8,4},{12,8},{5,1},{9,5},{13,9},{6,2},{10,6},{14,10},{7,3},{... | collective-permute-start | bytes 13832 | tf_op jit(solution)/shard_map/ppermute | solution.py:24
  104.2 1.3 %fusion.25 = f32[16,256,128]{2,1,0:T(8,128)S(1)} fusion(bf16[1,16,256,128]{3,2,1,0:T(8,128)(2,1)S(1)} %get-tuple-element.5, bf16[1,1,256,128]{3,2,1,0:T(8,128)(2,1)} %collective-permute-done.4, bf16[3,3,128,128]{3,2,1,0:T(8,128)(2,1)S(1)} %maximum_maximum_fusion.2), kind=kOutput, calls=%fused_computation.53 | convolution fusion | flops 134742016 | bytes 3244032 | tf_op jit(solution)/shard_map/sxyd,cd->sxyc/dot_general | solution.py:58
  106.0 5.1 %collective-permute-done.6 = bf16[1,18,1,128]{3,2,1,0:T(2,128)(2,1)S(1)} collective-permute-done((bf16[1,18,1,128]{3,2,1,0:T(2,128)(2,1)S(1)}, bf16[1,18,1,128]{3,2,1,0:T(2,128)(2,1)S(1)}, u32[]{:S(2)}, u32[]{:S(2)}) %collective-permute-start.6) | collective-permute-done | bytes 4640 | tf_op jit(solution)/shard_map/ppermute | solution.py:24
  111.0 1.5 %maximum_maximum_fusion = (bf16[1,18,257,128]{3,2,1,0:T(8,128)(2,1)S(1)}, bf16[1,18,257,128]{3,2,1,0:T(8,128)(2,1)S(1)}) fusion(bf16[1,1,256,128]{3,2,1,0:T(8,128)(2,1)S(1)} %collective-permute-done.5, bf16[1,16,256,128]{3,2,1,0:T(8,128)(2,1)S(1)} %get-tuple-element.5, bf16[1,1,256,128]{3,2,1,0:T(8,128)(2,1)} %collective-permute-done.4, ...), kind=kLoop, calls=%fused_computation.17 | loop fusion | flops 9474048 | bytes 3557376 | tf_op jit(solution)/shard_map/concatenate | solution.py:20
  114.8 2.2 %fusion.22 = bf16[1,16,256,128]{3,2,1,0:T(8,128)(2,1)} fusion(f32[16,256,128]{2,1,0:T(8,128)S(1)} %fusion.25, f32[16,256,128]{2,1,0:T(8,128)S(1)} %fusion.28, f32[16,256,128]{2,1,0:T(8,128)S(1)} %fusion.29, f32[16,256,128]{2,1,0:T(8,128)S(1)} %fusion.50, f32[16,256,128]{2,1,0:T(8,128)S(1)} %fusion.30, f32[16,256,128]{2,1,0:T(8,128)S(1)} %fusion.31, ...), kind=kOutput, calls=%fused_computation.48 | convolution fusion | flops 138936320 | bytes 18907136 | tf_op jit(solution)/shard_map/sxyd,cd->sxyc/dot_general | solution.py:58
  (55 shorter events, 12.1 us)
Async XLA Ops:
  0.6 9.1 %copy-start = (bf16[1,16,256,128]{3,2,1,0:T(8,128)(2,1)S(1)}, bf16[1,16,256,128]{3,2,1,0:T(8,128)(2,1)}, u32[]{:S(2)}) copy-start(bf16[1,16,256,128]{3,2,1,0:T(8,128)(2,1)} %param.5) | copy-start | bytes 3145732
  1.6 8.7 %collective-permute-start = (bf16[1,1,256,128]{3,2,1,0:T(8,128)(2,1)S(1)}, bf16[1,1,256,128]{3,2,1,0:T(8,128)(2,1)S(1)}, u32[]{:S(2)}, u32[]{:S(2)}) collective-permute-start(bf16[1,1,256,128]{3,2,1,0:T(8,128)(2,1)S(1)} %get-tuple-element.14), channel_id=1, source_target_pairs={{0,16},{16,32},{32,48},{48,64},{64,80},{80,96},{96,112},{112,128},... | collective-permute-start | bytes 196616 | tf_op jit(solution)/shard_map/ppermute | solution.py:22
  6.4 5.6 %collective-permute-start.1 = (bf16[1,1,256,128]{3,2,1,0:T(8,128)(2,1)S(1)}, bf16[1,1,256,128]{3,2,1,0:T(8,128)(2,1)S(1)}, u32[]{:S(2)}, u32[]{:S(2)}) collective-permute-start(bf16[1,1,256,128]{3,2,1,0:T(8,128)(2,1)S(1)} %get-tuple-element.15), channel_id=1, source_target_pairs={{16,0},{32,16},{48,32},{64,48},{80,64},{96,80},{112,96},{128,112},... | collective-permute-start | bytes 196616 | tf_op jit(solution)/shard_map/ppermute | solution.py:24
  9.5 0.7 copy-start.5
  12.1 13.3 %collective-permute-start.3 = (bf16[1,18,1,128]{3,2,1,0:T(2,128)(2,1)S(1)}, bf16[1,18,1,128]{3,2,1,0:T(2,128)(2,1)S(1)}, u32[]{:S(2)}, u32[]{:S(2)}) collective-permute-start(bf16[1,18,1,128]{3,2,1,0:T(2,128)(2,1)S(1)} %get-tuple-element.10), channel_id=1, source_target_pairs={{4,0},{8,4},{12,8},{5,1},{9,5},{13,9},{6,2},{10,6},{14,10},{7,3},{... | collective-permute-start | bytes 13832 | tf_op jit(solution)/shard_map/ppermute | solution.py:24
  17.9 6.2 %collective-permute-start.2 = (bf16[1,18,1,128]{3,2,1,0:T(2,128)(2,1)S(1)}, bf16[1,18,1,128]{3,2,1,0:T(2,128)(2,1)S(1)}, u32[]{:S(2)}, u32[]{:S(2)}) collective-permute-start(bf16[1,18,1,128]{3,2,1,0:T(2,128)(2,1)S(1)} %get-tuple-element.11), channel_id=1, source_target_pairs={{0,4},{4,8},{8,12},{1,5},{5,9},{9,13},{2,6},{6,10},{10,14},{3,7},{... | collective-permute-start | bytes 13832 | tf_op jit(solution)/shard_map/ppermute | solution.py:22
  25.8 1.2 %copy-start.1 = (bf16[1,16,256,128]{3,2,1,0:T(8,128)(2,1)S(1)}, bf16[1,16,256,128]{3,2,1,0:T(8,128)(2,1)}, u32[]{:S(2)}) copy-start(bf16[1,16,256,128]{3,2,1,0:T(8,128)(2,1)} %param.8) | copy-start | bytes 3145732
  79.1 17.7 %collective-permute-start.5 = (bf16[1,1,256,128]{3,2,1,0:T(8,128)(2,1)}, bf16[1,1,256,128]{3,2,1,0:T(8,128)(2,1)S(1)}, u32[]{:S(2)}, u32[]{:S(2)}) collective-permute-start(bf16[1,1,256,128]{3,2,1,0:T(8,128)(2,1)} %get-tuple-element.12), channel_id=1, source_target_pairs={{16,0},{32,16},{48,32},{64,48},{80,64},{96,80},{112,96},{128,112},... | collective-permute-start | bytes 196616 | tf_op jit(solution)/shard_map/ppermute | solution.py:24
  80.4 16.4 %collective-permute-start.4 = (bf16[1,1,256,128]{3,2,1,0:T(8,128)(2,1)}, bf16[1,1,256,128]{3,2,1,0:T(8,128)(2,1)}, u32[]{:S(2)}, u32[]{:S(2)}) collective-permute-start(bf16[1,1,256,128]{3,2,1,0:T(8,128)(2,1)} %get-tuple-element.13), channel_id=1, source_target_pairs={{0,16},{16,32},{32,48},{48,64},{64,80},{80,96},{96,112},{112,128},... | collective-permute-start | bytes 196616 | tf_op jit(solution)/shard_map/ppermute | solution.py:22
  91.7 3.2 %copy-start.2 = (f32[9,16,64]{2,1,0:T(8,128)S(1)}, f32[9,16,64]{2,1,0:T(8,128)}, u32[]{:S(2)}) copy-start(f32[9,16,64]{2,1,0:T(8,128)} %get-tuple-element.24) | copy-start | bytes 110596
  91.7 3.2 %copy-start.3 = (f32[9,16,64]{2,1,0:T(8,128)S(1)}, f32[9,16,64]{2,1,0:T(8,128)}, u32[]{:S(2)}) copy-start(f32[9,16,64]{2,1,0:T(8,128)} %get-tuple-element.25) | copy-start | bytes 110596
  91.7 3.2 %copy-start.4 = (f32[9,16,64]{2,1,0:T(8,128)S(1)}, f32[9,16,64]{2,1,0:T(8,128)}, u32[]{:S(2)}) copy-start(f32[9,16,64]{2,1,0:T(8,128)} %copy.42) | copy-start | bytes 110596
  97.5 8.4 %collective-permute-start.7 = (bf16[1,18,1,128]{3,2,1,0:T(2,128)(2,1)S(1)}, bf16[1,18,1,128]{3,2,1,0:T(2,128)(2,1)S(1)}, u32[]{:S(2)}, u32[]{:S(2)}) collective-permute-start(bf16[1,18,1,128]{3,2,1,0:T(2,128)(2,1)S(1)} %get-tuple-element.8), channel_id=1, source_target_pairs={{0,4},{4,8},{8,12},{1,5},{5,9},{9,13},{2,6},{6,10},{10,14},{3,7},{... | collective-permute-start | bytes 13832 | tf_op jit(solution)/shard_map/ppermute | solution.py:22
  102.1 8.9 %collective-permute-start.6 = (bf16[1,18,1,128]{3,2,1,0:T(2,128)(2,1)S(1)}, bf16[1,18,1,128]{3,2,1,0:T(2,128)(2,1)S(1)}, u32[]{:S(2)}, u32[]{:S(2)}) collective-permute-start(bf16[1,18,1,128]{3,2,1,0:T(2,128)(2,1)S(1)} %get-tuple-element.9), channel_id=1, source_target_pairs={{4,0},{8,4},{12,8},{5,1},{9,5},{13,9},{6,2},{10,6},{14,10},{7,3},{... | collective-permute-start | bytes 13832 | tf_op jit(solution)/shard_map/ppermute | solution.py:24

commit v2 on v0

v2 whole, which is shorter than its diff:
```python
import contextlib
import functools
import math

import jax
import jax.numpy as jnp
from jax import lax
from jax.experimental import pallas as pl
from jax.experimental.pallas import tpu as pltpu
from jax.sharding import PartitionSpec as P

MESH = pl.DeviceIdType.MESH
F32, BF16 = jnp.float32, jnp.bfloat16

NX, NZ, NH, NC, ND = 4, 8, 2, 2, 4
NYL = NH * ND
GX, GY = NX * NZ, NH * NC
TILES = 32
KEPT = TILES // (NC * NX)

SX, SY, W, CH, PAD = 16, 256, 128, 64, 16
PY = SY + 2 * PAD
PACK = 80


def place():
    gx, gy, d = lax.axis_index("gx"), lax.axis_index("gy"), lax.axis_index("dp")
    return gx // NZ, gx % NZ, gy // NC, gy % NC, d


def device(x, z, h, c, d):
    return {"gx": x * NZ + z, "gy": h * NC + c, "dp": d}


def gather_peer(x, z, h, c, d, j):
    return device((x + j // NC) % NX, z, h, (c + j) % NC, d)


def body(
    f_hbm, u_hbm, k_hbm, o_hbm, act, ig, gat,
    fx, ux, gx_ref, ft, mf, mb, acc, bacc, e32, ebf, rbuf, rcol, ucol, c32, gedge,
    v, cbuf, acc1, xbuf, acc2, ybuf, zbuf, kern, offs,
    lsem, hsem, csem, xsem, ysem, zsem, gsem,
):
    scopes = contextlib.ExitStack()

    def mark(name):
        scopes.close()
        scopes.enter_context(jax.named_scope(name))

    x, z, h, c, d = place()
    gx, gy = lax.axis_index("gx"), lax.axis_index("gy")
    y = h * ND + d

    def at(dx, dy):
        return {"gx": (gx + dx + GX) % GX, "gy": (gy + dy + GY) % GY, "dp": d}

    def remote(src, dst, sems, s, r, peer):
        return pltpu.make_async_remote_copy(
            src_ref=src, dst_ref=dst, send_sem=sems.at[0, s], recv_sem=sems.at[1, r],
            device_id=peer, device_id_type=MESH,
        )

    mark("setup")
    load_f = pltpu.make_async_copy(f_hbm, fx.at[2 : 2 + SX, PAD : PAD + SY], lsem.at[0])
    load_u = pltpu.make_async_copy(u_hbm, ux.at[1 : 1 + SX, PAD : PAD + SY], lsem.at[1])
    load_k = pltpu.make_async_copy(k_hbm, kern, lsem.at[2])
    load_o = pltpu.make_async_copy(o_hbm, offs, lsem.at[3])
    load_k.start()
    load_o.start()
    load_f.start()
    load_u.start()

    top, bottom, left, right = gx > 0, gx < GX - 1, gy > 0, gy < GY - 1

    def blank(ref, *where):
        ref[where] = jnp.zeros(ref[where].shape, ref.dtype)

    @pl.when(jnp.logical_not(top))
    def _():
        blank(fx, slice(0, 2), slice(PAD, PAD + SY))
        blank(ux, slice(0, 1), slice(PAD, PAD + SY))

    @pl.when(jnp.logical_not(bottom))
    def _():
        blank(fx, slice(SX + 2, SX + 4), slice(PAD, PAD + SY))
        blank(ux, slice(SX + 1, SX + 2), slice(PAD, PAD + SY))

    for side, there in ((0, left), (1, right)):
        for rows, other in ((slice(0, 48), True), (slice(48, 64), top), (slice(64, 80), bottom)):
            @pl.when(jnp.logical_not(jnp.logical_and(there, other)))
            def _(side=side, rows=rows):
                blank(rbuf, side, rows)

    barrier = pltpu.get_barrier_semaphore()
    around = [at(dx, dy) for dx in (-1, 0, 1) for dy in (-1, 0, 1) if dx or dy]
    others = [gather_peer(x, z, h, c, d, j) for j in range(1, NC * NX)]
    for k in range(1, NYL):
        other = (y + k) % NYL
        others.append(device(x, z, other // ND, c, other % ND))
    for k in range(1, NZ):
        others.append(device(x, (z + k) % NZ, h, c, d))
    for peer in around + others:
        pl.semaphore_signal(barrier, inc=1, device_id=peer, device_id_type=MESH)

    load_k.wait()
    load_o.wait()
    for a in range(3):
        for b in range(3):
            k0, k1, k2 = kern[a, b, 0], kern[a, b, 1], kern[a, b, 2]
            m = jnp.concatenate(
                [jnp.concatenate([k1, k0], axis=1), jnp.concatenate([k2, k1], axis=1)], axis=0
            )
            mf[a * W : (a + 1) * W, b * W : (b + 1) * W] = m
            mb[(2 - b) * W : (3 - b) * W, (2 - a) * W : (3 - a) * W] = m
    bias = jnp.concatenate([offs[...], offs[...]], axis=1)
    c32[...] = jnp.zeros_like(c32)
    e32[...] = jnp.zeros_like(e32)
    acc[...] = jnp.zeros_like(acc)
    bacc[...] = jnp.zeros_like(bacc)

    mark("rims")
    load_f.wait()
    load_u.wait()

    for r in range(SX):
        for side, base in ((0, PAD), (1, PAD + SY - 16)):
            near, second = (0, 1) if side == 0 else (15, 14)
            tf = fx[2 + r, base : base + 16].astype(F32)
            tu = ux[1 + r, base : base + 16].astype(F32)
            nf, sf, nu = tf[near : near + 1], tf[second : second + 1], tu[near : near + 1]
            e32[side, r : r + 1] = nf
            e32[side, 16 + r : 17 + r] = sf
            e32[side, 32 + r : 33 + r] = nu
            for corner, first, edge in ((48, 0, 0), (64, SX - 2, SX - 1)):
                if first <= r < first + 2:
                    k = corner + r - first
                    e32[side, k : k + 1] = nf
                    e32[side, k + 2 : k + 3] = sf
                if r == edge:
                    e32[side, corner + 4 : corner + 5] = nu
    ebf[...] = e32[...].astype(BF16)

    mark("barrier")
    pl.semaphore_wait(barrier, len(around) + len(others))

    mark("send_rims")
    rows_y = slice(PAD, PAD + SY)
    halos = [
        (top, -1, 0, f_hbm.at[0:2], fx.at[SX + 2 : SX + 4, rows_y], 0, 1),
        (top, -1, 0, u_hbm.at[0:1], ux.at[SX + 1 : SX + 2, rows_y], 2, 3),
        (bottom, 1, 0, f_hbm.at[SX - 2 : SX], fx.at[0:2, rows_y], 1, 0),
        (bottom, 1, 0, u_hbm.at[SX - 1 : SX], ux.at[0:1, rows_y], 3, 2),
        (left, 0, -1, ebf.at[0, 0:48], rbuf.at[1, 0:48], 4, 5),
        (right, 0, 1, ebf.at[1, 0:48], rbuf.at[0, 0:48], 5, 4),
        (jnp.logical_and(left, top), -1, -1, ebf.at[0, 48:64], rbuf.at[1, 64:80], 6, 9),
        (jnp.logical_and(left, bottom), 1, -1, ebf.at[0, 64:80], rbuf.at[1, 48:64], 7, 8),
        (jnp.logical_and(right, top), -1, 1, ebf.at[1, 48:64], rbuf.at[0, 64:80], 8, 7),
        (jnp.logical_and(right, bottom), 1, 1, ebf.at[1, 64:80], rbuf.at[0, 48:64], 9, 6),
    ]
    for there, dx, dy, src, dst, s, r in halos:
        @pl.when(there)
        def _(dx=dx, dy=dy, src=src, dst=dst, s=s, r=r):
            remote(src, dst, hsem, s, r, at(dx, dy)).start()

    mark("transpose")
    @pl.loop(2, SX + 2)
    def _(r):
        ft[r] = fx[r, PAD : PAD + SY].T

    arrivals = [
        (top, fx.at[0:2, rows_y], 0), (bottom, fx.at[SX + 2 : SX + 4, rows_y], 1),
        (top, ux.at[0:1, rows_y], 2), (bottom, ux.at[SX + 1 : SX + 2, rows_y], 3),
        (left, rbuf.at[0, 0:48], 4), (right, rbuf.at[1, 0:48], 5),
        (jnp.logical_and(left, top), rbuf.at[0, 48:64], 6),
        (jnp.logical_and(left, bottom), rbuf.at[0, 64:80], 7),
        (jnp.logical_and(right, top), rbuf.at[1, 48:64], 8),
        (jnp.logical_and(right, bottom), rbuf.at[1, 64:80], 9),
    ]
    mark("await_rims")
    for there, dst, s in arrivals:
        @pl.when(there)
        def _(dst=dst, s=s):
            remote(dst, dst, hsem, s, s, at(0, 1)).wait_recv()

    mark("place_rims")
    ft[1] = fx[1, PAD : PAD + SY].T
    ft[SX + 2] = fx[SX + 2, PAD : PAD + SY].T

    for side in range(2):
        got = rbuf[side].astype(F32)
        rcol[side, 0, 2 : SX + 2] = got[0:16]
        rcol[side, 1, 2 : SX + 2] = got[16:32]
        for k in range(2):
            for n, row in ((k, 48), (SX + 2 + k, 64)):
                rcol[side, 0, n : n + 1] = got[row + k : row + k + 1]
                rcol[side, 1, n : n + 1] = got[row + 2 + k : row + 3 + k]
        ucol[side, 1 : SX + 1] = got[32:48]
        ucol[side, 0:1] = got[52:53]
        ucol[side, SX + 1 : SX + 2] = got[68:69]
        near, second = (15, 14) if side == 0 else (0, 1)
        base = 0 if side == 0 else PAD + SY
        for r in range(SX + 4):
            c32[r, near : near + 1] = rcol[side, 0, r : r + 1]
            c32[r, second : second + 1] = rcol[side, 1, r : r + 1]
        fx[:, base : base + PAD] = c32[...].astype(BF16)
        c32[:, second : second + 1] = jnp.zeros((SX + 4, 1, W), F32)
        for r in range(SX + 2):
            c32[r, near : near + 1] = ucol[side, r : r + 1]
        ux[:, base : base + PAD] = c32[0 : SX + 2].astype(BF16)
        c32[:, near : near + 1] = jnp.zeros((SX + 4, 1, W), F32)

    mark("forward")
    spot = lax.broadcasted_iota(jnp.int32, (SY, W), 0)

    @pl.loop(0, SX + 2)
    def _(r):
        window = jnp.concatenate([fx[r], fx[r + 1], fx[r + 2]], axis=1)
        p = jnp.dot(window, mf[...], preferred_element_type=F32)
        pre = (
            pltpu.roll(p[:, :W], 1, 0) + p[:, W : 2 * W] + pltpu.roll(p[:, 2 * W :], PY - 1, 0) + bias
        )
        sigma = jax.nn.sigmoid(pre)
        grad = (ux[r].astype(F32) * sigma * (1.0 + pre * (1.0 - sigma))).astype(BF16)
        gx_ref[r] = grad

        @pl.when(jnp.logical_and(r >= 1, r <= SX))
        def _():
            act[r - 1] = (pre * sigma)[PAD : PAD + SY].astype(BF16)
            g32 = grad.astype(F32)
            inner = g32[PAD : PAD + SY]
            bacc[...] += inner.reshape(SY // 8, 8, W).sum(axis=0)
            gedge[0, pl.ds(r - 1, 1)] = inner[0:1]
            gedge[1, pl.ds(r - 1, 1)] = inner[SY - 1 : SY]
            after = pltpu.roll(g32, PY - 1, 0)[PAD : PAD + SY]
            before = pltpu.roll(g32, 1, 0)[PAD : PAD + SY]
            after = jnp.where(spot == SY - 1, 0.0, after).astype(BF16)
            before = jnp.where(spot == 0, 0.0, before).astype(BF16)
            rhs = jnp.concatenate([after, grad[PAD : PAD + SY], before], axis=1)
            lhs = jnp.concatenate([ft[r], ft[r + 1], ft[r + 2]], axis=0)
            acc[...] += jnp.dot(lhs, rhs, preferred_element_type=F32)

    mark("rim_columns")

    for side in range(2):
        lhs = jnp.concatenate([rcol[side, 0, a + 1 : a + 1 + SX] for a in range(3)], axis=1)
        part = lax.dot_general(
            lhs.astype(BF16), gedge[side].astype(BF16), (((0,), (0,)), ((), ())), preferred_element_type=F32
        )
        acc[:, 2 * side * W : (2 * side + 1) * W] += part

    mark("pack")
    lane = lax.broadcasted_iota(jnp.int32, (CH, W), 1)

    def put(j, block):
        for dd in range(ND):
            for half in range(2):
                t = 2 * j + half
                v[t // (NX * KEPT), (t // KEPT) % NX, dd, t % KEPT] = block[
                    16 * dd + 8 * half : 16 * dd + 8 * half + 8
                ]

    lows = []
    for a in range(3):
        for b in range(3):
            t = acc[a * W : (a + 1) * W, b * W : (b + 1) * W].T
            turned = pltpu.roll(t[CH:], CH, 1)
            put(3 * a + b, t[:CH] + jnp.where(lane < CH, turned, 0.0))
            lows.append((t[CH:], turned))
    total = jnp.sum(bacc[...], axis=0, keepdims=True)
    col = jnp.broadcast_to(total, (W, W)).T
    lows.append((None, col[:CH] + col[CH:]))
    for k in range(5):
        put(9 + k, jnp.where(lane < CH, lows[2 * k][0], lows[2 * k + 1][1]))
    for t in range(28, TILES):
        for dd in range(ND):
            v[t // (NX * KEPT), (t // KEPT) % NX, dd, t % KEPT] = jnp.zeros((8, W), F32)

    def input_rows(first, last):
        @pl.loop(first, last)
        def _(r):
            window = jnp.concatenate([gx_ref[r], gx_ref[r + 1], gx_ref[r + 2]], axis=1)
            p = lax.dot_general(
                window, mb[...], (((1,), (1,)), ((), ())), preferred_element_type=F32
            )
            out = pltpu.roll(p[:, :W], 1, 0) + p[:, W : 2 * W] + pltpu.roll(p[:, 2 * W :], PY - 1, 0)
            ig[r] = out[PAD : PAD + SY].astype(BF16)

    sent = []
    mark("sum_cores")
    first = remote(v.at[1 - c], cbuf, csem, 0, 0, device(x, z, h, 1 - c, d))
    first.start()
    sent.append(first)
    first.wait_recv()
    acc1[...] = v[c] + cbuf[...]

    mark("sum_x")
    along = []
    for k in range(1, NX):
        other = (x + k) % NX
        copy = remote(acc1.at[other], xbuf.at[k - 1], xsem, k - 1, k - 1, device(other, z, h, c, d))
        copy.start()
        along.append(copy)
    sent += along
    input_rows(0, 6)
    for copy in along:
        copy.wait_recv()
    acc2[...] = acc1[x] + xbuf[0] + xbuf[1] + xbuf[2]

    mark("sum_y")
    ybuf[y] = acc2[d]
    for k in range(1, NYL):
        other = (y + k) % NYL
        copy = remote(
            acc2.at[other % ND], ybuf.at[y], ysem, k - 1, k - 1, device(x, z, other // ND, c, other % ND)
        )
        copy.start()
        sent.append(copy)
    input_rows(6, 11)
    for k in range(1, NYL):
        other = (y + NYL - k) % NYL
        slot = ybuf.at[other]
        remote(slot, slot, ysem, k - 1, k - 1, device(x, z, other // ND, c, other % ND)).wait_recv()
    part = ybuf[0]
    for k in range(1, NYL):
        part = part + ybuf[k]
    zbuf[z] = part

    mark("sum_z")
    for k in range(1, NZ):
        copy = remote(zbuf.at[z], zbuf.at[z], zsem, k - 1, k - 1, device(x, (z + k) % NZ, h, c, d))
        copy.start()
        sent.append(copy)
    input_rows(11, SX)
    for k in range(1, NZ):
        other = (z + NZ - k) % NZ
        slot = zbuf.at[other]
        remote(slot, slot, zsem, k - 1, k - 1, device(x, other, h, c, d)).wait_recv()
    part = zbuf[0]
    for k in range(1, NZ):
        part = part + zbuf[k]
    gat[c, x] = part

    mark("gather")
    for j in range(1, NC * NX):
        copy = remote(gat.at[c, x], gat.at[c, x], gsem, j - 1, j - 1, gather_peer(x, z, h, c, d, j))
        copy.start()
        sent.append(copy)
    for j in range(1, NC * NX):
        px, pc = (x + NX - j // NC) % NX, (c + NC - j % NC) % NC
        slot = gat.at[pc, px]
        remote(slot, slot, gsem, j - 1, j - 1, device(px, z, h, pc, d)).wait_recv()

    mark("drain")
    for copy in sent:
        copy.wait_send()
    for there, dx, dy, src, dst, s, r in halos:
        @pl.when(there)
        def _(dx=dx, dy=dy, src=src, dst=dst, s=s, r=r):
            remote(src, dst, hsem, s, r, at(dx, dy)).wait_send()
    scopes.close()


def finish(scale, act_in, ig_in, gat, exps, act_hbm, ig_hbm, kg_ref, bg_ref, lsem):
    copies = [
        pltpu.make_async_copy(act_in, act_hbm, lsem.at[0]),
        pltpu.make_async_copy(ig_in, ig_hbm, lsem.at[1]),
    ]
    for copy in copies:
        copy.start()

    def tile(j):
        t = 2 * j
        return jnp.concatenate(
            [gat[t // (NX * KEPT), (t // KEPT) % NX, t % KEPT + i] for i in range(2)], axis=0
        )

    def scaled(value, a, b, k):
        factor = jnp.exp2(jnp.full((16, CH), exps[a, b, k], jnp.int32).astype(F32)) * scale
        kg_ref[a, b, k] = (value * factor).astype(BF16)

    for j in range(9):
        both = tile(j)
        pair = tile(9 + j // 2)
        low = pair if j % 2 == 0 else pltpu.roll(pair, CH, 1)
        scaled(low[:, :CH], j // 3, j % 3, 0)
        scaled(both[:, :CH], j // 3, j % 3, 1)
        scaled(pltpu.roll(both, CH, 1)[:, :CH], j // 3, j % 3, 2)
    column = pltpu.roll(tile(13), CH, 1)[:, :16]
    same = lax.broadcasted_iota(jnp.int32, (16, 16), 0) == lax.broadcasted_iota(jnp.int32, (16, 16), 1)
    bg_ref[...] = jnp.sum(jnp.where(same, column, 0.0), axis=0, keepdims=True) * scale
    for copy in copies:
        copy.wait()


def local(features, kernel, offsets, upstream, grad_exponents):
    count = 4 * GX * GY * SX * SY * 2
    vmem, anywhere = pltpu.VMEM, pl.BlockSpec(memory_space=pl.ANY)
    hbm = pl.BlockSpec(memory_space=pltpu.HBM)
    in_vmem = pl.BlockSpec(memory_space=pltpu.VMEM)
    dma = pltpu.SemaphoreType.DMA
    activation, input_grad, gathered = pl.pallas_call(
        body,
        out_shape=(
            jax.ShapeDtypeStruct((SX, SY, W), BF16),
            jax.ShapeDtypeStruct((SX, SY, W), BF16),
            jax.ShapeDtypeStruct((NC, NX, KEPT, 8, W), F32),
        ),
        in_specs=[hbm, hbm, hbm, hbm],
        out_specs=(in_vmem, in_vmem, in_vmem),
        scratch_shapes=[
            vmem((SX + 4, PY, W), BF16),
            vmem((SX + 2, PY, W), BF16),
            vmem((SX + 2, PY, W), BF16),
            vmem((SX + 4, W, SY), BF16),
            vmem((3 * W, 3 * W), BF16),
            vmem((3 * W, 3 * W), BF16),
            vmem((3 * W, 3 * W), F32),
            vmem((8, W), F32),
            vmem((2, PACK, W), F32),
            vmem((2, PACK, W), BF16),
            vmem((2, PACK, W), BF16),
            vmem((2, 2, 24, W), F32),
            vmem((2, 24, W), F32),
            vmem((SX + 4, PAD, W), F32),
            vmem((2, SX, W), F32),
            vmem((NC, NX, ND, KEPT, 8, W), F32),
            vmem((NX, ND, KEPT, 8, W), F32),
            vmem((NX, ND, KEPT, 8, W), F32),
            vmem((NX - 1, ND, KEPT, 8, W), F32),
            vmem((ND, KEPT, 8, W), F32),
            vmem((NYL, KEPT, 8, W), F32),
            vmem((NZ, KEPT, 8, W), F32),
            vmem((3, 3, 3, CH, CH), BF16),
            vmem((1, CH), F32),
            dma((4,)),
            dma((2, 10)),
            dma((2, 1)),
            dma((2, NX - 1)),
            dma((2, NYL - 1)),
            dma((2, NZ - 1)),
            dma((2, NC * NX - 1)),
        ],
        compiler_params=pltpu.CompilerParams(
            collective_id=0, has_side_effects=True, vmem_limit_bytes=24 << 20
        ),
    )(
        pltpu.with_memory_space_constraint(features.reshape(SX, SY, W), pltpu.HBM),
        pltpu.with_memory_space_constraint(upstream.reshape(SX, SY, W), pltpu.HBM),
        pltpu.with_memory_space_constraint(kernel, pltpu.HBM),
        pltpu.with_memory_space_constraint(offsets.reshape(1, CH), pltpu.HBM),
    )
    activation, input_grad, kernel_grad, bias_grad = pl.pallas_call(
        functools.partial(finish, 1.0 / math.sqrt(count)),
        out_shape=(
            jax.ShapeDtypeStruct((SX, SY, W), BF16),
            jax.ShapeDtypeStruct((SX, SY, W), BF16),
            jax.ShapeDtypeStruct((3, 3, 3, 16, CH), BF16),
            jax.ShapeDtypeStruct((1, 16), F32),
        ),
        in_specs=[in_vmem, in_vmem, in_vmem, pl.BlockSpec(memory_space=pltpu.SMEM)],
        out_specs=(hbm, hbm, in_vmem, in_vmem),
        scratch_shapes=[dma((2,))],
        compiler_params=pltpu.CompilerParams(vmem_limit_bytes=24 << 20),
    )(activation, input_grad, gathered, grad_exponents)
    kernel_grad = kernel_grad.swapaxes(3, 4)
    return (
        activation.reshape(features.shape),
        input_grad.reshape(features.shape),
        kernel_grad,
        bias_grad.reshape(16),
    )


def solution(mesh):
    placed = (P("dp", "gx", "gy", None), P(), P(), P("dp", "gx", "gy", None), P())
    return jax.shard_map(
        local,
        mesh=mesh,
        in_specs=placed,
        out_specs=(
            P("dp", "gx", "gy", None),
            P("dp", "gx", "gy", None),
            P(None, None, None, None, "dp"),
            P("dp"),
        ),
        check_vma=False,
    )
```

time: 1930 us -> 60.8 us (0.03)
  waiting for transfers between devices: 1420 us -> 0 us
  blocking collectives: 419 us -> 0 us
  Pallas kernels: 0 us -> 60 us
  matrix products: 35.5 us -> 0 us
  starting transfers between devices: 27.8 us -> 0 us
    psum x1 -> x0, waiting for transfers between devices: 1420 us -> none  [local(): tap_grad, bias_sum = lax.psum((tap_grad, bias_sum), ('gx', 'gy'))]
    psum x1 -> x0, blocking collectives: 409 us -> none  [local(): tap_grad, bias_sum = lax.psum((tap_grad, bias_sum), ('gx', 'gy'))]
    pallas_call x0 -> x2, Pallas kernels: none -> 60 us  [the longest x1 57.4 us: local(): pl.pallas_call(body, out_shape=(jax.ShapeDtypeStruct((SX, SY, W), BF16),...]
    dot_general x27 -> x0, matrix products: 35.5 us -> none  [the longest x9 21.9 us: backward_conv(): jnp.einsum('sxyd,cd->sxyc', window, matrices[shift_x, shift_y], preferred...]
    ppermute x8 -> x0, starting transfers between devices: 27.7 us -> none  [the longest x4 15.7 us: extended(): lax.ppermute(tail, axis, [(i, (i + 1) % count) for i in range(ends)])]
  transfers between devices with their start and end apart: 10 -> 0, of which waited for: 2 -> 0; matrix products, arithmetic and copies ran while one was open for 2% -> 0% of each run, Pallas kernels for 0% -> 0%
where the time goes in v2:
time: 60.8 us; the launch traced here: 60.7 us
  Pallas kernels  60 us (99%)
  between operations  0.66 us (1%)
    pallas_call x1, Pallas kernels, local(): pl.pallas_call(body, out_shape=(jax.ShapeDtypeStruct((SX, SY, W), BF16),...  57.4 us
    pallas_call x1, Pallas kernels, local(): pl.pallas_call(functools.partial(finish, 1.0 / math.sqrt(count)), out_sha...  2.62 us

profile of v2, /device:TPU:1, one launch (start us, length us, event | category | flops | bytes accessed | tf_op | source)
XLA Modules:
  0.0 60.7 jit_solution(14357563982812530099)
XLA Ops:
  0.6 0.0 copy-start
  0.6 57.4 %shard_map.84 = (bf16[16,256,128]{2,1,0:T(8,128)(2,1)S(1)}, bf16[16,256,128]{2,1,0:T(8,128)(2,1)S(1)}, f32[2,4,4,8,128]{4,3,2,1,0:T(8,128)S(1)}) custom-call(bf16[16,256,128]{2,1,0:T(8,128)(2,1)} %bitcast.7, bf16[16,256,128]{2,1,0:T(8,128)(2,1)} %bitcast.8, bf16[3,3,3,64,64]{4,3,2,1,0:T(8,128)(2,1)} %k_hbm.1, f32[1,64]{1,0:T(1,128)} %bitcast.9), custom_call_target="tpu_custom_call" | custom-call | tf_op jit(solution)/shard_map/pallas_call | solution.py:402
  58.0 0.0 copy-done
  58.0 2.6 %shard_map.85 = (bf16[16,256,128]{2,1,0:T(8,128)(2,1)}, bf16[16,256,128]{2,1,0:T(8,128)(2,1)}, bf16[3,3,3,16,64]{4,3,2,1,0:T(8,128)(2,1)}, f32[1,16]{1,0:T(1,128)}) custom-call(bf16[16,256,128]{2,1,0:T(8,128)(2,1)S(1)} %get-tuple-element.11.act_in, bf16[16,256,128]{2,1,0:T(8,128)(2,1)S(1)} %get-tuple-element.12.ig_in, ...), custom_call_target="tpu_custom_call" | custom-call | tf_op jit(solution)/shard_map/pallas_call | solution.py:453
Async XLA Ops:
  0.6 57.4 %copy-start = (s32[3,3,3]{2,1,0:T(4,128)S(1)}, s32[3,3,3]{2,1,0:T(4,128)}, u32[]{:S(2)}) copy-start(s32[3,3,3]{2,1,0:T(4,128)} %exps.1) | copy-start | bytes 328

commit v3 on v2

--- a/solution.py
+++ b/solution.py
@@ -15,8 +15,6 @@
 NX, NZ, NH, NC, ND = 4, 8, 2, 2, 4
 NYL = NH * ND
 GX, GY = NX * NZ, NH * NC
-TILES = 32
-KEPT = TILES // (NC * NX)
 
 SX, SY, W, CH, PAD = 16, 256, 128, 64, 16
 PY = SY + 2 * PAD
@@ -38,7 +36,7 @@
 
 def body(
     f_hbm, u_hbm, k_hbm, o_hbm, act, ig, gat,
-    fx, ux, gx_ref, ft, mf, mb, acc, bacc, e32, ebf, rbuf, rcol, ucol, c32, gedge,
+    fx, ux, gx_ref, ft, mf, mb, acc, bacc, e32, ebf, rbuf, rcol, ucol, gedge,
     v, cbuf, acc1, xbuf, acc2, ybuf, zbuf, kern, offs,
     lsem, hsem, csem, xsem, ysem, zsem, gsem,
 ):
@@ -72,25 +70,6 @@
     load_u.start()
 
     top, bottom, left, right = gx > 0, gx < GX - 1, gy > 0, gy < GY - 1
-
-    def blank(ref, *where):
-        ref[where] = jnp.zeros(ref[where].shape, ref.dtype)
-
-    @pl.when(jnp.logical_not(top))
-    def _():
-        blank(fx, slice(0, 2), slice(PAD, PAD + SY))
-        blank(ux, slice(0, 1), slice(PAD, PAD + SY))
-
-    @pl.when(jnp.logical_not(bottom))
-    def _():
-        blank(fx, slice(SX + 2, SX + 4), slice(PAD, PAD + SY))
-        blank(ux, slice(SX + 1, SX + 2), slice(PAD, PAD + SY))
-
-    for side, there in ((0, left), (1, right)):
-        for rows, other in ((slice(0, 48), True), (slice(48, 64), top), (slice(64, 80), bottom)):
-            @pl.when(jnp.logical_not(jnp.logical_and(there, other)))
-            def _(side=side, rows=rows):
-                blank(rbuf, side, rows)
 
     barrier = pltpu.get_barrier_semaphore()
     around = [at(dx, dy) for dx in (-1, 0, 1) for dy in (-1, 0, 1) if dx or dy]
@@ -103,25 +82,32 @@
     for peer in around + others:
         pl.semaphore_signal(barrier, inc=1, device_id=peer, device_id_type=MESH)
 
-    load_k.wait()
-    load_o.wait()
-    for a in range(3):
-        for b in range(3):
-            k0, k1, k2 = kern[a, b, 0], kern[a, b, 1], kern[a, b, 2]
-            m = jnp.concatenate(
-                [jnp.concatenate([k1, k0], axis=1), jnp.concatenate([k2, k1], axis=1)], axis=0
-            )
-            mf[a * W : (a + 1) * W, b * W : (b + 1) * W] = m
-            mb[(2 - b) * W : (3 - b) * W, (2 - a) * W : (3 - a) * W] = m
-    bias = jnp.concatenate([offs[...], offs[...]], axis=1)
-    c32[...] = jnp.zeros_like(c32)
-    e32[...] = jnp.zeros_like(e32)
-    acc[...] = jnp.zeros_like(acc)
-    bacc[...] = jnp.zeros_like(bacc)
+    mark("barrier")
+    pl.semaphore_wait(barrier, len(around) + len(others))
+
+    mark("send_rims")
+    rows_y = slice(PAD, PAD + SY)
+    halos = [
+        (top, -1, 0, f_hbm.at[0:2], fx.at[SX + 2 : SX + 4, rows_y], 0, 1),
+        (top, -1, 0, u_hbm.at[0:1], ux.at[SX + 1 : SX + 2, rows_y], 2, 3),
+        (bottom, 1, 0, f_hbm.at[SX - 2 : SX], fx.at[0:2, rows_y], 1, 0),
+        (bottom, 1, 0, u_hbm.at[SX - 1 : SX], ux.at[0:1, rows_y], 3, 2),
+        (left, 0, -1, ebf.at[0, 0:48], rbuf.at[1, 0:48], 4, 5),
+        (right, 0, 1, ebf.at[1, 0:48], rbuf.at[0, 0:48], 5, 4),
+        (jnp.logical_and(left, top), -1, -1, ebf.at[0, 48:64], rbuf.at[1, 64:80], 6, 9),
+        (jnp.logical_and(left, bottom), 1, -1, ebf.at[0, 64:80], rbuf.at[1, 48:64], 7, 8),
+        (jnp.logical_and(right, top), -1, 1, ebf.at[1, 48:64], rbuf.at[0, 64:80], 8, 7),
+        (jnp.logical_and(right, bottom), 1, 1, ebf.at[1, 64:80], rbuf.at[0, 48:64], 9, 6),
+    ]
+    for there, dx, dy, src, dst, s, r in halos[:4]:
+        @pl.when(there)
+        def _(dx=dx, dy=dy, src=src, dst=dst, s=s, r=r):
+            remote(src, dst, hsem, s, r, at(dx, dy)).start()
 
     mark("rims")
     load_f.wait()
     load_u.wait()
+    e32[...] = jnp.zeros_like(e32)
 
     for r in range(SX):
         for side, base in ((0, PAD), (1, PAD + SY - 16)):
@@ -141,27 +127,44 @@
                     e32[side, corner + 4 : corner + 5] = nu
     ebf[...] = e32[...].astype(BF16)
 
-    mark("barrier")
-    pl.semaphore_wait(barrier, len(around) + len(others))
-
-    mark("send_rims")
-    rows_y = slice(PAD, PAD + SY)
-    halos = [
-        (top, -1, 0, f_hbm.at[0:2], fx.at[SX + 2 : SX + 4, rows_y], 0, 1),
-        (top, -1, 0, u_hbm.at[0:1], ux.at[SX + 1 : SX + 2, rows_y], 2, 3),
-        (bottom, 1, 0, f_hbm.at[SX - 2 : SX], fx.at[0:2, rows_y], 1, 0),
-        (bottom, 1, 0, u_hbm.at[SX - 1 : SX], ux.at[0:1, rows_y], 3, 2),
-        (left, 0, -1, ebf.at[0, 0:48], rbuf.at[1, 0:48], 4, 5),
-        (right, 0, 1, ebf.at[1, 0:48], rbuf.at[0, 0:48], 5, 4),
-        (jnp.logical_and(left, top), -1, -1, ebf.at[0, 48:64], rbuf.at[1, 64:80], 6, 9),
-        (jnp.logical_and(left, bottom), 1, -1, ebf.at[0, 64:80], rbuf.at[1, 48:64], 7, 8),
-        (jnp.logical_and(right, top), -1, 1, ebf.at[1, 48:64], rbuf.at[0, 64:80], 8, 7),
-        (jnp.logical_and(right, bottom), 1, 1, ebf.at[1, 64:80], rbuf.at[0, 48:64], 9, 6),
-    ]
-    for there, dx, dy, src, dst, s, r in halos:
+    for there, dx, dy, src, dst, s, r in halos[4:]:
         @pl.when(there)
         def _(dx=dx, dy=dy, src=src, dst=dst, s=s, r=r):
             remote(src, dst, hsem, s, r, at(dx, dy)).start()
+
+    mark("matrices")
+    def blank(ref, *where):
+        ref[where] = jnp.zeros(ref[where].shape, ref.dtype)
+
+    @pl.when(jnp.logical_not(top))
+    def _():
+        blank(fx, slice(0, 2), slice(PAD, PAD + SY))
+        blank(ux, slice(0, 1), slice(PAD, PAD + SY))
+
+    @pl.when(jnp.logical_not(bottom))
+    def _():
+        blank(fx, slice(SX + 2, SX + 4), slice(PAD, PAD + SY))
+        blank(ux, slice(SX + 1, SX + 2), slice(PAD, PAD + SY))
+
+    for side, there in ((0, left), (1, right)):
+        for rows, other in ((slice(0, 48), True), (slice(48, 64), top), (slice(64, 80), bottom)):
+            @pl.when(jnp.logical_not(jnp.logical_and(there, other)))
+            def _(side=side, rows=rows):
+                blank(rbuf, side, rows)
+
+    load_k.wait()
+    load_o.wait()
+    for a in range(3):
+        for b in range(3):
+            k0, k1, k2 = kern[a, b, 0], kern[a, b, 1], kern[a, b, 2]
+            m = jnp.concatenate(
+                [jnp.concatenate([k1, k0], axis=1), jnp.concatenate([k2, k1], axis=1)], axis=0
+            )
+            mf[a * W : (a + 1) * W, b * W : (b + 1) * W] = m
+            mb[(2 - b) * W : (3 - b) * W, (2 - a) * W : (3 - a) * W] = m
+    bias = jnp.concatenate([offs[...], offs[...]], axis=1)
+    acc[...] = jnp.zeros_like(acc)
+    bacc[...] = jnp.zeros_like(bacc)
 
     mark("transpose")
     @pl.loop(2, SX + 2)
@@ -198,23 +201,29 @@
         ucol[side, 1 : SX + 1] = got[32:48]
         ucol[side, 0:1] = got[52:53]
         ucol[side, SX + 1 : SX + 2] = got[68:69]
-        near, second = (15, 14) if side == 0 else (0, 1)
         base = 0 if side == 0 else PAD + SY
+        sub = lax.broadcasted_iota(jnp.int32, (8, W), 0)
+        near, second = (7, 6) if side == 0 else (0, 1)
+        empty = jnp.zeros((8, W), F32)
+
+        def spread(rows):
+            return jnp.broadcast_to(rows, (8, W))
+
+        def padded(half):
+            return jnp.concatenate([empty, half] if side == 0 else [half, empty], axis=0).astype(BF16)
+
         for r in range(SX + 4):
-            c32[r, near : near + 1] = rcol[side, 0, r : r + 1]
-            c32[r, second : second + 1] = rcol[side, 1, r : r + 1]
-        fx[:, base : base + PAD] = c32[...].astype(BF16)
-        c32[:, second : second + 1] = jnp.zeros((SX + 4, 1, W), F32)
+            other = jnp.where(sub == second, spread(rcol[side, 1, r : r + 1]), 0.0)
+            half = jnp.where(sub == near, spread(rcol[side, 0, r : r + 1]), other)
+            fx[r, base : base + PAD] = padded(half)
         for r in range(SX + 2):
-            c32[r, near : near + 1] = ucol[side, r : r + 1]
-        ux[:, base : base + PAD] = c32[0 : SX + 2].astype(BF16)
-        c32[:, near : near + 1] = jnp.zeros((SX + 4, 1, W), F32)
+            half = jnp.where(sub == near, spread(ucol[side, r : r + 1]), 0.0)
+            ux[r, base : base + PAD] = padded(half)
 
     mark("forward")
     spot = lax.broadcasted_iota(jnp.int32, (SY, W), 0)
 
-    @pl.loop(0, SX + 2)
-    def _(r):
+    def forward_row(r):
         window = jnp.concatenate([fx[r], fx[r + 1], fx[r + 2]], axis=1)
         p = jnp.dot(window, mf[...], preferred_element_type=F32)
         pre = (
@@ -223,22 +232,32 @@
         sigma = jax.nn.sigmoid(pre)
         grad = (ux[r].astype(F32) * sigma * (1.0 + pre * (1.0 - sigma))).astype(BF16)
         gx_ref[r] = grad
-
-        @pl.when(jnp.logical_and(r >= 1, r <= SX))
-        def _():
-            act[r - 1] = (pre * sigma)[PAD : PAD + SY].astype(BF16)
-            g32 = grad.astype(F32)
-            inner = g32[PAD : PAD + SY]
-            bacc[...] += inner.reshape(SY // 8, 8, W).sum(axis=0)
-            gedge[0, pl.ds(r - 1, 1)] = inner[0:1]
-            gedge[1, pl.ds(r - 1, 1)] = inner[SY - 1 : SY]
-            after = pltpu.roll(g32, PY - 1, 0)[PAD : PAD + SY]
-            before = pltpu.roll(g32, 1, 0)[PAD : PAD + SY]
-            after = jnp.where(spot == SY - 1, 0.0, after).astype(BF16)
-            before = jnp.where(spot == 0, 0.0, before).astype(BF16)
-            rhs = jnp.concatenate([after, grad[PAD : PAD + SY], before], axis=1)
-            lhs = jnp.concatenate([ft[r], ft[r + 1], ft[r + 2]], axis=0)
+        return pre, sigma, grad
+
+    def weight_row(r):
+        pre, sigma, grad = forward_row(r)
+        act[r - 1] = (pre * sigma)[PAD : PAD + SY].astype(BF16)
+        g32 = grad.astype(F32)
+        inner = g32[PAD : PAD + SY]
+        bacc[...] += inner.reshape(SY // 8, 8, W).sum(axis=0)
+        gedge[0, pl.ds(r - 1, 1)] = inner[0:1]
+        gedge[1, pl.ds(r - 1, 1)] = inner[SY - 1 : SY]
+        after = pltpu.roll(g32, PY - 1, 0)[PAD : PAD + SY]
+        before = pltpu.roll(g32, 1, 0)[PAD : PAD + SY]
+        after = jnp.where(spot == SY - 1, 0.0, after).astype(BF16)
+        before = jnp.where(spot == 0, 0.0, before).astype(BF16)
+        return jnp.concatenate([after, grad[PAD : PAD + SY], before], axis=1)
+
+    @pl.loop(0, SX // 16)
+    def _(step):
+        for k in range(0, 16, 4):
+            r = step * 16 + k + 1
+            rhs = jnp.concatenate([weight_row(r + n) for n in range(4)], axis=0)
+            lhs = jnp.concatenate(
+                [jnp.concatenate([ft[r + n + a] for n in range(4)], axis=1) for a in range(3)], axis=0
+            )
             acc[...] += jnp.dot(lhs, rhs, preferred_element_type=F32)
+
 
     mark("rim_columns")
 
@@ -253,28 +272,23 @@
     lane = lax.broadcasted_iota(jnp.int32, (CH, W), 1)
 
     def put(j, block):
-        for dd in range(ND):
-            for half in range(2):
-                t = 2 * j + half
-                v[t // (NX * KEPT), (t // KEPT) % NX, dd, t % KEPT] = block[
-                    16 * dd + 8 * half : 16 * dd + 8 * half + 8
-                ]
-
-    lows = []
+        m = j // 2
+        v[m // NX, m % NX, j % 2] = block
+
+    highs = []
     for a in range(3):
         for b in range(3):
-            t = acc[a * W : (a + 1) * W, b * W : (b + 1) * W].T
+            t = acc[a * W : (a + 1) * W, b * W : (b + 1) * W]
             turned = pltpu.roll(t[CH:], CH, 1)
             put(3 * a + b, t[:CH] + jnp.where(lane < CH, turned, 0.0))
-            lows.append((t[CH:], turned))
+            highs.append((t[CH:], turned))
     total = jnp.sum(bacc[...], axis=0, keepdims=True)
-    col = jnp.broadcast_to(total, (W, W)).T
-    lows.append((None, col[:CH] + col[CH:]))
+    total = jnp.broadcast_to(total, (CH, W))
+    highs.append((None, total + pltpu.roll(total, CH, 1)))
     for k in range(5):
-        put(9 + k, jnp.where(lane < CH, lows[2 * k][0], lows[2 * k + 1][1]))
-    for t in range(28, TILES):
-        for dd in range(ND):
-            v[t // (NX * KEPT), (t // KEPT) % NX, dd, t % KEPT] = jnp.zeros((8, W), F32)
+        put(9 + k, jnp.where(lane < CH, highs[2 * k][0], highs[2 * k + 1][1]))
+    for j in (14, 15):
+        put(j, jnp.zeros((CH, W), F32))
 
     def input_rows(first, last):
         @pl.loop(first, last)
@@ -302,10 +316,15 @@
         copy.start()
         along.append(copy)
     sent += along
-    input_rows(0, 6)
+    forward_row(0)
+    forward_row(SX + 1)
+    input_rows(0, 5)
     for copy in along:
         copy.wait_recv()
-    acc2[...] = acc1[x] + xbuf[0] + xbuf[1] + xbuf[2]
+    pair = (acc1[x] + xbuf[0] + xbuf[1] + xbuf[2]).reshape(W, W).T
+    for dd in range(ND):
+        acc2[dd, 0] = pair[16 * dd : 16 * dd + 16]
+        acc2[dd, 1] = pair[CH + 16 * dd : CH + 16 * dd + 16]
 
     mark("sum_y")
     ybuf[y] = acc2[d]
@@ -316,7 +335,7 @@
         )
         copy.start()
         sent.append(copy)
-    input_rows(6, 11)
+    input_rows(5, 11)
     for k in range(1, NYL):
         other = (y + NYL - k) % NYL
         slot = ybuf.at[other]
@@ -369,24 +388,20 @@
     for copy in copies:
         copy.start()
 
-    def tile(j):
-        t = 2 * j
-        return jnp.concatenate(
-            [gat[t // (NX * KEPT), (t // KEPT) % NX, t % KEPT + i] for i in range(2)], axis=0
-        )
+    def tile(j, half):
+        m = j // 2
+        block = gat[m // NX, m % NX, half]
+        return block if j % 2 == 0 else pltpu.roll(block, CH, 1)
 
     def scaled(value, a, b, k):
         factor = jnp.exp2(jnp.full((16, CH), exps[a, b, k], jnp.int32).astype(F32)) * scale
         kg_ref[a, b, k] = (value * factor).astype(BF16)
 
     for j in range(9):
-        both = tile(j)
-        pair = tile(9 + j // 2)
-        low = pair if j % 2 == 0 else pltpu.roll(pair, CH, 1)
-        scaled(low[:, :CH], j // 3, j % 3, 0)
-        scaled(both[:, :CH], j // 3, j % 3, 1)
-        scaled(pltpu.roll(both, CH, 1)[:, :CH], j // 3, j % 3, 2)
-    column = pltpu.roll(tile(13), CH, 1)[:, :16]
+        scaled(tile(j, 1)[:, :CH], j // 3, j % 3, 0)
+        scaled(tile(j, 0)[:, :CH], j // 3, j % 3, 1)
+        scaled(tile(9 + j // 2, j % 2)[:, :CH], j // 3, j % 3, 2)
+    column = tile(13, 1)[:, :16]
     same = lax.broadcasted_iota(jnp.int32, (16, 16), 0) == lax.broadcasted_iota(jnp.int32, (16, 16), 1)
     bg_ref[...] = jnp.sum(jnp.where(same, column, 0.0), axis=0, keepdims=True) * scale
     for copy in copies:
@@ -404,7 +419,7 @@
         out_shape=(
             jax.ShapeDtypeStruct((SX, SY, W), BF16),
             jax.ShapeDtypeStruct((SX, SY, W), BF16),
-            jax.ShapeDtypeStruct((NC, NX, KEPT, 8, W), F32),
+            jax.ShapeDtypeStruct((NC, NX, 2, 16, W), F32),
         ),
         in_specs=[hbm, hbm, hbm, hbm],
         out_specs=(in_vmem, in_vmem, in_vmem),
@@ -422,15 +437,14 @@
             vmem((2, PACK, W), BF16),
             vmem((2, 2, 24, W), F32),
             vmem((2, 24, W), F32),
-            vmem((SX + 4, PAD, W), F32),
             vmem((2, SX, W), F32),
-            vmem((NC, NX, ND, KEPT, 8, W), F32),
-            vmem((NX, ND, KEPT, 8, W), F32),
-            vmem((NX, ND, KEPT, 8, W), F32),
-            vmem((NX - 1, ND, KEPT, 8, W), F32),
-            vmem((ND, KEPT, 8, W), F32),
-            vmem((NYL, KEPT, 8, W), F32),
-            vmem((NZ, KEPT, 8, W), F32),
+            vmem((NC, NX, 2, CH, W), F32),
+            vmem((NX, 2, CH, W), F32),
+            vmem((NX, 2, CH, W), F32),
+            vmem((NX - 1, 2, CH, W), F32),
+            vmem((ND, 2, 16, W), F32),
+            vmem((NYL, 2, 16, W), F32),
+            vmem((NZ, 2, 16, W), F32),
             vmem((3, 3, 3, CH, CH), BF16),
             vmem((1, CH), F32),
             dma((4,)),

time: 60.8 us -> 54.1 us (0.89)
  Pallas kernels: 60 us -> 53.3 us
    pallas_call x1, Pallas kernels: 57.4 us -> 50.7 us  [local(): pl.pallas_call(body, out_shape=(jax.ShapeDtypeStruct((SX, SY, W), BF16),...]
where the time goes in v3:
time: 54.1 us; the launch traced here: 53.9 us
  Pallas kernels  53.3 us (99%)
  between operations  0.66 us (1%)
    pallas_call x1, Pallas kernels, local(): pl.pallas_call(body, out_shape=(jax.ShapeDtypeStruct((SX, SY, W), BF16),...  50.7 us
    pallas_call x1, Pallas kernels, local(): pl.pallas_call(functools.partial(finish, 1.0 / math.sqrt(count)), out_sha...  2.62 us

profile of v3, /device:TPU:1, one launch (start us, length us, event | category | flops | bytes accessed | tf_op | source)
XLA Modules:
  0.0 53.9 jit_solution(16222491580633509904)
XLA Ops:
  0.6 0.0 copy-start
  0.6 50.7 %shard_map.84 = (bf16[16,256,128]{2,1,0:T(8,128)(2,1)S(1)}, bf16[16,256,128]{2,1,0:T(8,128)(2,1)S(1)}, f32[2,4,2,16,128]{4,3,2,1,0:T(8,128)S(1)}) custom-call(bf16[16,256,128]{2,1,0:T(8,128)(2,1)} %bitcast.7, bf16[16,256,128]{2,1,0:T(8,128)(2,1)} %bitcast.8, bf16[3,3,3,64,64]{4,3,2,1,0:T(8,128)(2,1)} %k_hbm.1, f32[1,64]{1,0:T(1,128)} %bitcast.9), custom_call_target="tpu_custom_call" | custom-call | tf_op jit(solution)/shard_map/pallas_call | solution.py:417
  51.3 0.0 copy-done
  51.3 2.6 %shard_map.85 = (bf16[16,256,128]{2,1,0:T(8,128)(2,1)}, bf16[16,256,128]{2,1,0:T(8,128)(2,1)}, bf16[3,3,3,16,64]{4,3,2,1,0:T(8,128)(2,1)}, f32[1,16]{1,0:T(1,128)}) custom-call(bf16[16,256,128]{2,1,0:T(8,128)(2,1)S(1)} %get-tuple-element.11.act_in, bf16[16,256,128]{2,1,0:T(8,128)(2,1)S(1)} %get-tuple-element.12.ig_in, ...), custom_call_target="tpu_custom_call" | custom-call | tf_op jit(solution)/shard_map/pallas_call | solution.py:467
Async XLA Ops:
  0.6 50.7 %copy-start = (s32[3,3,3]{2,1,0:T(4,128)S(1)}, s32[3,3,3]{2,1,0:T(4,128)}, u32[]{:S(2)}) copy-start(s32[3,3,3]{2,1,0:T(4,128)} %exps.1) | copy-start | bytes 328

commit v4 on v3

--- a/solution.py
+++ b/solution.py
@@ -37,7 +37,7 @@
 def body(
     f_hbm, u_hbm, k_hbm, o_hbm, act, ig, gat,
     fx, ux, gx_ref, ft, mf, mb, acc, bacc, e32, ebf, rbuf, rcol, ucol, gedge,
-    v, cbuf, acc1, xbuf, acc2, ybuf, zbuf, kern, offs,
+    v, cbuf, acc1, acc1b, xbuf, acc2, ybuf, zbuf, kern, offs,
     lsem, hsem, csem, xsem, ysem, zsem, gsem,
 ):
     scopes = contextlib.ExitStack()
@@ -307,12 +307,13 @@
     sent.append(first)
     first.wait_recv()
     acc1[...] = v[c] + cbuf[...]
+    acc1b[...] = acc1[...].astype(BF16)
 
     mark("sum_x")
     along = []
     for k in range(1, NX):
         other = (x + k) % NX
-        copy = remote(acc1.at[other], xbuf.at[k - 1], xsem, k - 1, k - 1, device(other, z, h, c, d))
+        copy = remote(acc1b.at[other], xbuf.at[k - 1], xsem, k - 1, k - 1, device(other, z, h, c, d))
         copy.start()
         along.append(copy)
     sent += along
@@ -321,10 +322,10 @@
     input_rows(0, 5)
     for copy in along:
         copy.wait_recv()
-    pair = (acc1[x] + xbuf[0] + xbuf[1] + xbuf[2]).reshape(W, W).T
+    pair = (acc1[x] + xbuf[0].astype(F32) + xbuf[1].astype(F32) + xbuf[2].astype(F32)).reshape(W, W).T
     for dd in range(ND):
-        acc2[dd, 0] = pair[16 * dd : 16 * dd + 16]
-        acc2[dd, 1] = pair[CH + 16 * dd : CH + 16 * dd + 16]
+        acc2[dd, 0] = pair[16 * dd : 16 * dd + 16].astype(BF16)
+        acc2[dd, 1] = pair[CH + 16 * dd : CH + 16 * dd + 16].astype(BF16)
 
     mark("sum_y")
     ybuf[y] = acc2[d]
@@ -340,10 +341,10 @@
         other = (y + NYL - k) % NYL
         slot = ybuf.at[other]
         remote(slot, slot, ysem, k - 1, k - 1, device(x, z, other // ND, c, other % ND)).wait_recv()
-    part = ybuf[0]
+    part = ybuf[0].astype(F32)
     for k in range(1, NYL):
-        part = part + ybuf[k]
-    zbuf[z] = part
+        part = part + ybuf[k].astype(F32)
+    zbuf[z] = part.astype(BF16)
 
     mark("sum_z")
     for k in range(1, NZ):
@@ -355,10 +356,15 @@
         other = (z + NZ - k) % NZ
         slot = zbuf.at[other]
         remote(slot, slot, zsem, k - 1, k - 1, device(x, other, h, c, d)).wait_recv()
-    part = zbuf[0]
+    part = zbuf[0].astype(F32)
     for k in range(1, NZ):
-        part = part + zbuf[k]
-    gat[c, x] = part
+        part = part + zbuf[k].astype(F32)
+    whole = part.astype(BF16)
+    rest = (part - whole.astype(F32)).astype(BF16)
+    lanes = lax.broadcasted_iota(jnp.int32, (2, 16, W), 2)
+    halves = lax.broadcasted_iota(jnp.int32, (2, 16, W), 0)
+    low_bias = jnp.logical_and(jnp.logical_and(lanes >= CH + 32, halves == 1), 4 * c + x == 6)
+    gat[c, x] = jnp.where(low_bias, rest.astype(F32), whole.astype(F32)).astype(BF16)
 
     mark("gather")
     for j in range(1, NC * NX):
@@ -390,7 +396,7 @@
 
     def tile(j, half):
         m = j // 2
-        block = gat[m // NX, m % NX, half]
+        block = gat[m // NX, m % NX, half].astype(F32)
         return block if j % 2 == 0 else pltpu.roll(block, CH, 1)
 
     def scaled(value, a, b, k):
@@ -401,7 +407,8 @@
         scaled(tile(j, 1)[:, :CH], j // 3, j % 3, 0)
         scaled(tile(j, 0)[:, :CH], j // 3, j % 3, 1)
         scaled(tile(9 + j // 2, j % 2)[:, :CH], j // 3, j % 3, 2)
-    column = tile(13, 1)[:, :16]
+    last = tile(13, 1)
+    column = last[:, :16] + pltpu.roll(last, W - 32, 1)[:, :16]
     same = lax.broadcasted_iota(jnp.int32, (16, 16), 0) == lax.broadcasted_iota(jnp.int32, (16, 16), 1)
     bg_ref[...] = jnp.sum(jnp.where(same, column, 0.0), axis=0, keepdims=True) * scale
     for copy in copies:
@@ -419,7 +426,7 @@
         out_shape=(
             jax.ShapeDtypeStruct((SX, SY, W), BF16),
             jax.ShapeDtypeStruct((SX, SY, W), BF16),
-            jax.ShapeDtypeStruct((NC, NX, 2, 16, W), F32),
+            jax.ShapeDtypeStruct((NC, NX, 2, 16, W), BF16),
         ),
         in_specs=[hbm, hbm, hbm, hbm],
         out_specs=(in_vmem, in_vmem, in_vmem),
@@ -441,10 +448,11 @@
             vmem((NC, NX, 2, CH, W), F32),
             vmem((NX, 2, CH, W), F32),
             vmem((NX, 2, CH, W), F32),
-            vmem((NX - 1, 2, CH, W), F32),
-            vmem((ND, 2, 16, W), F32),
-            vmem((NYL, 2, 16, W), F32),
-            vmem((NZ, 2, 16, W), F32),
+            vmem((NX, 2, CH, W), BF16),
+            vmem((NX - 1, 2, CH, W), BF16),
+            vmem((ND, 2, 16, W), BF16),
+            vmem((NYL, 2, 16, W), BF16),
+            vmem((NZ, 2, 16, W), BF16),
             vmem((3, 3, 3, CH, CH), BF16),
             vmem((1, CH), F32),
             dma((4,)),

time: 54.1 us -> 50.7 us (0.937)
  Pallas kernels: 53.3 us -> 49.9 us
    pallas_call x1, Pallas kernels: 50.7 us -> 47.3 us  [local(): pl.pallas_call(body, out_shape=(jax.ShapeDtypeStruct((SX, SY, W), BF16),...]
where the time goes in v4:
time: 50.7 us; the launch traced here: 50.6 us
  Pallas kernels  49.9 us (98%)
  between operations  0.66 us (1%)
    pallas_call x1, Pallas kernels, local(): pl.pallas_call(body, out_shape=(jax.ShapeDtypeStruct((SX, SY, W), BF16),...  47.3 us
    pallas_call x1, Pallas kernels, local(): pl.pallas_call(functools.partial(finish, 1.0 / math.sqrt(count)), out_sha...  2.62 us

profile of v4, /device:TPU:1, one launch (start us, length us, event | category | flops | bytes accessed | tf_op | source)
XLA Modules:
  0.0 50.6 jit_solution(6141425210325461087)
XLA Ops:
  0.6 0.0 copy-start
  0.6 47.3 %shard_map.84 = (bf16[16,256,128]{2,1,0:T(8,128)(2,1)S(1)}, bf16[16,256,128]{2,1,0:T(8,128)(2,1)S(1)}, bf16[2,4,2,16,128]{4,3,2,1,0:T(8,128)(2,1)S(1)}) custom-call(bf16[16,256,128]{2,1,0:T(8,128)(2,1)} %bitcast.7, bf16[16,256,128]{2,1,0:T(8,128)(2,1)} %bitcast.8, bf16[3,3,3,64,64]{4,3,2,1,0:T(8,128)(2,1)} %k_hbm.1, f32[1,64]{1,0:T(1,128)} %bitcast.9), custom_call_target="tpu_custom_call" | custom-call | tf_op jit(solution)/shard_map/pallas_call | solution.py:424
  48.0 0.0 copy-done
  48.0 2.6 %shard_map.85 = (bf16[16,256,128]{2,1,0:T(8,128)(2,1)}, bf16[16,256,128]{2,1,0:T(8,128)(2,1)}, bf16[3,3,3,16,64]{4,3,2,1,0:T(8,128)(2,1)}, f32[1,16]{1,0:T(1,128)}) custom-call(bf16[16,256,128]{2,1,0:T(8,128)(2,1)S(1)} %get-tuple-element.11.act_in, bf16[16,256,128]{2,1,0:T(8,128)(2,1)S(1)} %get-tuple-element.12.ig_in, ...), custom_call_target="tpu_custom_call" | custom-call | tf_op jit(solution)/shard_map/pallas_call | solution.py:475
Async XLA Ops:
  0.6 47.3 %copy-start = (s32[3,3,3]{2,1,0:T(4,128)S(1)}, s32[3,3,3]{2,1,0:T(4,128)}, u32[]{:S(2)}) copy-start(s32[3,3,3]{2,1,0:T(4,128)} %exps.1) | copy-start | bytes 328

commit v5 on v4

--- a/solution.py
+++ b/solution.py
@@ -19,6 +19,8 @@
 SX, SY, W, CH, PAD = 16, 256, 128, 64, 16
 PY = SY + 2 * PAD
 PACK = 80
+
+FAR_FIRST = (4, 3, 5, 2, 6, 1, 7)
 
 
 def place():
@@ -127,7 +129,7 @@
                     e32[side, corner + 4 : corner + 5] = nu
     ebf[...] = e32[...].astype(BF16)
 
-    for there, dx, dy, src, dst, s, r in halos[4:]:
+    for there, dx, dy, src, dst, s, r in halos[6:] + halos[4:6]:
         @pl.when(there)
         def _(dx=dx, dy=dy, src=src, dst=dst, s=s, r=r):
             remote(src, dst, hsem, s, r, at(dx, dy)).start()
@@ -311,7 +313,7 @@
 
     mark("sum_x")
     along = []
-    for k in range(1, NX):
+    for k in (2, 1, 3):
         other = (x + k) % NX
         copy = remote(acc1b.at[other], xbuf.at[k - 1], xsem, k - 1, k - 1, device(other, z, h, c, d))
         copy.start()
@@ -329,7 +331,7 @@
 
     mark("sum_y")
     ybuf[y] = acc2[d]
-    for k in range(1, NYL):
+    for k in FAR_FIRST:
         other = (y + k) % NYL
         copy = remote(
             acc2.at[other % ND], ybuf.at[y], ysem, k - 1, k - 1, device(x, z, other // ND, c, other % ND)
@@ -347,7 +349,7 @@
     zbuf[z] = part.astype(BF16)
 
     mark("sum_z")
-    for k in range(1, NZ):
+    for k in FAR_FIRST:
         copy = remote(zbuf.at[z], zbuf.at[z], zsem, k - 1, k - 1, device(x, (z + k) % NZ, h, c, d))
         copy.start()
         sent.append(copy)
@@ -367,7 +369,7 @@
     gat[c, x] = jnp.where(low_bias, rest.astype(F32), whole.astype(F32)).astype(BF16)
 
     mark("gather")
-    for j in range(1, NC * NX):
+    for j in (4, 5, 2, 3, 6, 7, 1):
         copy = remote(gat.at[c, x], gat.at[c, x], gsem, j - 1, j - 1, gather_peer(x, z, h, c, d, j))
         copy.start()
         sent.append(copy)

time: 50.7 us -> 49.8 us (0.982)
  Pallas kernels: 49.9 us -> 49 us
    pallas_call x1, Pallas kernels: 47.3 us -> 46.3 us  [local(): pl.pallas_call(body, out_shape=(jax.ShapeDtypeStruct((SX, SY, W), BF16),...]
where the time goes in v5:
time: 49.8 us; the launch traced here: 49.6 us
  Pallas kernels  49 us (98%)
  between operations  0.66 us (1%)
    pallas_call x1, Pallas kernels, local(): pl.pallas_call(body, out_shape=(jax.ShapeDtypeStruct((SX, SY, W), BF16),...  46.3 us
    pallas_call x1, Pallas kernels, local(): pl.pallas_call(functools.partial(finish, 1.0 / math.sqrt(count)), out_sha...  2.62 us

profile of v5, /device:TPU:1, one launch (start us, length us, event | category | flops | bytes accessed | tf_op | source)
XLA Modules:
  0.0 49.6 jit_solution(18191423106739422030)
XLA Ops:
  0.6 0.0 copy-start
  0.6 46.3 %shard_map.84 = (bf16[16,256,128]{2,1,0:T(8,128)(2,1)S(1)}, bf16[16,256,128]{2,1,0:T(8,128)(2,1)S(1)}, bf16[2,4,2,16,128]{4,3,2,1,0:T(8,128)(2,1)S(1)}) custom-call(bf16[16,256,128]{2,1,0:T(8,128)(2,1)} %bitcast.7, bf16[16,256,128]{2,1,0:T(8,128)(2,1)} %bitcast.8, bf16[3,3,3,64,64]{4,3,2,1,0:T(8,128)(2,1)} %k_hbm.1, f32[1,64]{1,0:T(1,128)} %bitcast.9), custom_call_target="tpu_custom_call" | custom-call | tf_op jit(solution)/shard_map/pallas_call | solution.py:426
  47.0 0.0 copy-done
  47.0 2.6 %shard_map.85 = (bf16[16,256,128]{2,1,0:T(8,128)(2,1)}, bf16[16,256,128]{2,1,0:T(8,128)(2,1)}, bf16[3,3,3,16,64]{4,3,2,1,0:T(8,128)(2,1)}, f32[1,16]{1,0:T(1,128)}) custom-call(bf16[16,256,128]{2,1,0:T(8,128)(2,1)S(1)} %get-tuple-element.11.act_in, bf16[16,256,128]{2,1,0:T(8,128)(2,1)S(1)} %get-tuple-element.12.ig_in, ...), custom_call_target="tpu_custom_call" | custom-call | tf_op jit(solution)/shard_map/pallas_call | solution.py:477
Async XLA Ops:
  0.6 46.4 %copy-start = (s32[3,3,3]{2,1,0:T(4,128)S(1)}, s32[3,3,3]{2,1,0:T(4,128)}, u32[]{:S(2)}) copy-start(s32[3,3,3]{2,1,0:T(4,128)} %exps.1) | copy-start | bytes 328
